TPU v7x, 128 devices: a whole 4x4x4 slice. The times are simulated.
128 devices in a mesh: seq: 8 (over y, core), enc: 16 (over z, x).
Axes of the slice: x: 4, y: 4, z: 4, core: 2. Of those that a mesh axis runs over, the one named last changes fastest.
Arguments:
- text: bfloat16 [10240, 4096], P('seq', 'enc'), may hold values from -16 to 16
- visual: bfloat16 [5120, 4096], P(('seq', 'enc')), may hold values from -6 to 6
- gain: bfloat16 [4096], P('enc'), may hold values from 0.25 to 1.75
- w_query: bfloat16 [4096, 4096], P('enc'), may hold values from -1 to 1
- w_keyval: bfloat16 [4096, 2048], P('enc'), may hold values from -1 to 1
- image_count: int32 [32], replicated, may hold values from 1 to 256, 5120 in all
- text_gap: int32 [33], replicated, may hold values from 1 to 256, 5120 in all
Outputs:
- attended: bfloat16 [10240, 4096], P('seq', 'enc')
Inputs may be any that keep to these rules, and one draw needn't show every extreme that they name: `image_count`: 32 counts that sum to 5120; the largest is exactly 256. `text_gap`: 33 text runs that sum to 5120; the largest is exactly 256.
All inputs are finite; a program needn't handle non-finite values.
Results may differ from a plain program's by a relative error of at most 0.025.
Values may be sent and summed in bfloat16 or wider, within the bound.
A program may use at most 256 MiB of HBM per device.

v0:
```python
import math

import jax
import jax.numpy as jnp
from jax import lax
from jax.sharding import PartitionSpec as P

HD = 128


eps = 1e-05


def swapped(value, axis, bit):
    return lax.ppermute(value, axis, [(i, i ^ 1 << bit) for i in range(lax.axis_size(axis))])


def layout(image_count, text_gap):
    offsets = jnp.cumsum(image_count) - image_count
    starts = jnp.cumsum(text_gap[:-1]) + offsets
    return (offsets, starts)


def span_lookup(positions, starts, span_ends):
    inside = (positions[:, None] >= starts[None, :]) & (positions[:, None] < span_ends[None, :])
    frame_ids = jnp.arange(starts.shape[0], dtype=jnp.int32) + 1
    span_of = jnp.sum(jnp.where(inside, frame_ids[None, :], 0), axis=1) - 1
    return (inside, span_of)


def per_device(text, visual, gain, w_query, w_keyval, image_count, text_gap):
    tok_rows = text.shape[0]
    feature_slice = text.shape[1]
    vis_rows = visual.shape[0]
    seq_count = lax.axis_size("seq")
    enc_count = lax.axis_size("enc")
    seq_index = lax.axis_index("seq")
    enc_index = lax.axis_index("enc")
    device_total = seq_count * enc_count
    offsets, starts = layout(image_count, text_gap)
    span_ends = starts + image_count
    device = seq_index * enc_count + enc_index
    own_rows = jnp.arange(vis_rows, dtype=jnp.int32) * device_total + device
    owner_hit = (own_rows[:, None] >= offsets[None, :]) & (
        own_rows[:, None] < (offsets + image_count)[None, :]
    )
    target_pos = jnp.sum(jnp.where(owner_hit, (starts - offsets)[None, :], 0), axis=1) + own_rows
    target_block = target_pos // tok_rows
    bound_for = target_block[None, :] == jnp.arange(seq_count, dtype=jnp.int32)[:, None]
    pieces = jnp.transpose(visual.reshape(vis_rows, enc_count, feature_slice), (1, 0, 2))
    outgoing = jnp.where(bound_for[:, None, :, None], pieces[None], jnp.zeros((), jnp.bfloat16))
    arrived = lax.all_to_all(
        outgoing.reshape(seq_count * enc_count, vis_rows, feature_slice),
        ("seq", "enc"),
        split_axis=0,
        concat_axis=0,
        tiled=True,
    )
    arrived = arrived.reshape(-1, feature_slice)
    positions = seq_index * tok_rows + jnp.arange(tok_rows, dtype=jnp.int32)
    inside, query_span = span_lookup(positions, starts, span_ends)
    row_index = jnp.sum(jnp.where(inside, (offsets - starts)[None, :], 0), axis=1) + positions
    is_visual = query_span >= 0
    token_index = jnp.where(is_visual, row_index, 0)
    arrival_row = token_index % device_total * vis_rows + token_index // device_total
    picked = jnp.take(arrived, arrival_row, axis=0)
    stream = jnp.where(is_visual[:, None], picked, text)
    gathered, gain_all = (
        lax.all_gather(stream, "enc", axis=1, tiled=True),
        lax.all_gather(gain, "enc", axis=0, tiled=True),
    )
    widened = gathered.astype(jnp.float32)
    mean_square = jnp.mean(widened * widened, axis=1, keepdims=True)
    normed = (
        widened * lax.rsqrt(mean_square + eps) * gain_all.astype(jnp.float32)[None, :]
    ).astype(jnp.bfloat16)
    query_cols, keyval_cols = (
        lax.all_to_all(w_query, "enc", split_axis=1, concat_axis=0, tiled=True),
        lax.all_to_all(w_keyval, "enc", split_axis=1, concat_axis=0, tiled=True),
    )
    query = jnp.dot(normed, query_cols, preferred_element_type=jnp.float32).astype(jnp.bfloat16)
    keyval = jnp.dot(normed, keyval_cols, preferred_element_type=jnp.float32).astype(jnp.bfloat16)
    partner = swapped(keyval, "enc", 0)
    holds_keys = enc_index % 2 == 0
    key_part = jnp.where(holds_keys, keyval, partner)
    value_part = jnp.where(holds_keys, partner, keyval)
    keyval = jnp.concatenate((key_part, value_part), axis=1)
    local_heads = query.shape[1] // HD
    kv_heads = keyval.shape[1] // (2 * HD)
    group_size = local_heads // kv_heads
    grouped = query.reshape(tok_rows, kv_heads, group_size, HD)
    score_scale = 1.0 / HD**0.5
    initial = (
        jnp.full((kv_heads, group_size, tok_rows), -1e30, jnp.float32),
        jnp.zeros((kv_heads, group_size, tok_rows), jnp.float32),
        jnp.zeros((kv_heads, group_size, tok_rows, HD), jnp.float32),
    )
    running = initial
    portion = lax.all_gather(keyval, "seq", axis=0, tiled=True)
    first_row = jnp.int32(0)
    row_count = portion.shape[0]
    stride = math.gcd(row_count, 1024)
    for index_in in range(row_count // stride):
        key_block = portion[index_in * stride : (index_in + 1) * stride].reshape(
            stride, kv_heads, 2, HD
        )
        key_pos = first_row + index_in * stride + jnp.arange(stride, dtype=jnp.int32)
        unused, key_span = span_lookup(key_pos, starts, span_ends)
        visible = (key_pos[None, :] <= positions[:, None]) | (
            query_span[:, None] == key_span[None, :]
        ) & (query_span[:, None] >= 0)
        update_run_max, update_run_sum, update_totals = running
        scores = (
            jnp.einsum(
                "tkgd,skd->kgts", grouped, key_block[:, :, 0, :], preferred_element_type=jnp.float32
            )
            * score_scale
        )
        scores = jnp.where(visible[None, None], scores, -1e30)
        new_max = jnp.maximum(update_run_max, jnp.max(scores, axis=-1))
        weights = jnp.where(visible[None, None], jnp.exp(scores - new_max[..., None]), 0.0)
        rescale = jnp.exp(update_run_max - new_max)
        new_sum = update_run_sum * rescale + jnp.sum(weights, axis=-1)
        added = jnp.einsum(
            "kgts,skd->kgtd",
            weights.astype(jnp.bfloat16),
            key_block[:, :, 1, :],
            preferred_element_type=jnp.float32,
        )
        running = (new_max, new_sum, update_totals * rescale[..., None] + added)
    run_max, run_sum, totals = running
    result = totals / run_sum[..., None]
    return (
        jnp.transpose(result, (2, 0, 1, 3)).reshape(tok_rows, local_heads * HD).astype(jnp.bfloat16)
    )


def solution(mesh):
    in_specs = (
        P("seq", "enc"),
        P(("seq", "enc"), None),
        P("enc"),
        P("enc", None),
        P("enc", None),
        P(),
        P(),
    )
    out_specs = P("seq", "enc")
    return jax.shard_map(
        per_device, mesh=mesh, in_specs=in_specs, out_specs=out_specs, check_vma=False
    )
```

profile of v0, /device:TPU:1, one launch (start us, length us, event | category | flops | bytes accessed | tf_op | source)
XLA Modules:
  0.0 432.3 jit_solution(9255251804578692653)
XLA Ops:
  6.5 0.7 slice_bitcast_fusion.40
  7.3 0.1 reduce.20
  7.5 0.7 copy.153
  8.3 0.1 reduce.21
  8.4 0.7 fusion.200
  9.2 1.0 copy.220
  10.3 1.9 bitcast_select_fusion.10
  12.3 11.5 %all-to-all-start = ((bf16[128,40,256]{2,1,0:T(8,128)(2,1)}), bf16[128,40,256]{2,1,0:T(8,128)(2,1)S(1)}, u32[]{:S(2)}, u32[]{:S(2)}) async-start(bf16[128,40,256]{2,1,0:T(8,128)(2,1)} %bitcast_select_fusion.10), calls=%async_computation | async-start | bytes 5242880 | tf_op jit(solution)/shard_map/all_to_all | solution.py:52
  23.8 0.1 select_reduce_fusion
  24.1 34.6 %all-to-all-done = bf16[128,40,256]{2,1,0:T(8,128)(2,1)S(1)} async-done(((bf16[128,40,256]{2,1,0:T(8,128)(2,1)}), bf16[128,40,256]{2,1,0:T(8,128)(2,1)S(1)}, u32[]{:S(2)}, u32[]{:S(2)}) %all-to-all-start) | async-done | bytes 2621472 | tf_op jit(solution)/shard_map/all_to_all | solution.py:52
  58.7 4.1 gather_fusion
  62.7 2.6 select_select_fusion
  65.4 2.3 copy.155
  67.7 4.0 all-to-all-start.1
  71.7 32.7 %all-gather = bf16[16,1,256]{2,1,0:T(2,128)(2,1)S(1)} all-gather(bf16[1,1,256]{2,1,0:T(2,128)(2,1)S(1)} %reshape.1892), channel_id=1, replica_groups=mesh['seq'=8,'enc'=16] {'enc'}, dimensions={0}, use_global_device_ids=true | all-gather | bytes 8704 | tf_op jit(solution)/shard_map/all_gather | solution.py:70
  104.4 4.1 copy.158
  108.5 3.9 all-to-all-start.2
  112.5 1.3 copy.156
  113.8 66.1 %all-gather.4.cloned.1.call-done = bf16[1280,4096]{1,0:T(8,128)(2,1)} async-done(((bf16[1280,256]{1,0:T(8,128)(2,1)}), bf16[1280,4096]{1,0:T(8,128)(2,1)}) %all-gather.4.cloned.1.call-update) | async-done | bytes 10485776 | tf_op jit(solution)/shard_map/all_gather | solution.py:69
  180.0 6.2 %fusion = f32[1280]{0:T(1024)S(1)} fusion(bf16[1280,4096]{1,0:T(8,128)(2,1)} %all-gather.4.cloned.1.call-done), kind=kLoop, calls=%fused_computation.3 | loop fusion | flops 15727360 | bytes 10490880 | tf_op jit(solution)/shard_map/reduce_sum | solution.py:73
  186.2 0.7 copy-done
  186.9 5.0 %fusion.138 = bf16[1280,128]{0,1:T(8,128)(2,1)S(1)} fusion(bf16[4096,128]{1,0:T(8,128)(2,1)} %bitcast.451, bf16[1280,4096]{1,0:T(8,128)(2,1)S(1)} %copy-done, f32[4096]{0:T(1024)S(1)} %bitcast.475, f32[1280]{0:T(1024)S(1)} %add_rsqrt_fusion), kind=kOutput, calls=%fused_computation.120 | convolution fusion | flops 1363312640 | bytes 11883520 | tf_op jit(solution)/shard_map/dot_general | solution.py:82
  191.9 1.4 collective-permute-start
  193.3 0.3 select_reduce_fusion.2
  193.7 6.0 %collective-permute-done = bf16[1280,128]{0,1:T(8,128)(2,1)S(1)} collective-permute-done((bf16[1280,128]{0,1:T(8,128)(2,1)S(1)}, bf16[1280,128]{0,1:T(8,128)(2,1)S(1)}, u32[]{:S(2)}, u32[]{:S(2)}) %collective-permute-start) | collective-permute-done | bytes 327712 | tf_op jit(solution)/shard_map/ppermute | solution.py:15
  199.7 0.9 pad_maximum_fusion
  200.7 13.4 %and_or_fusion.8 = (pred[1280,1024]{0,1:T(8,128)(4,1)}, pred[1280,1024]{0,1:T(8,128)(4,1)}, pred[1280,1024]{0,1:T(8,128)(4,1)}, pred[1280,1024]{0,1:T(8,128)(4,1...) fusion(s32[1280]{0:T(1024)S(1)} %broadcast_add_fusion, ...), kind=kLoop, calls=%fused_computation.95 | loop fusion | flops 41943040 | bytes 10562816 | tf_op jit(solution)/shard_map/or | solution.py:109
  214.2 3.8 and_or_fusion
  218.0 2.4 copy.159
  220.4 8.8 %fusion.135 = bf16[1280,256]{0,1:T(8,128)(2,1)} fusion(bf16[4096,256]{1,0:T(8,128)(2,1)} %bitcast.449, bf16[1280,4096]{1,0:T(8,128)(2,1)} %all-gather.4.cloned.1.call-done, f32[4096]{0:T(1024)S(1)} %bitcast.476, f32[1280]{0:T(1024)S(1)} %add_rsqrt_fusion), kind=kOutput, calls=%fused_computation.119 | convolution fusion | flops 2705653760 | bytes 13259776 | tf_op jit(solution)/shard_map/dot_general | solution.py:81
  229.2 9.9 %all-gather.6.cloned.1.call-done = bf16[10240,256]{0,1:T(8,128)(2,1)} async-done(((bf16[1280,256]{0,1:T(8,128)(2,1)}), bf16[10240,256]{0,1:T(8,128)(2,1)}) %all-gather.6.cloned.1.call-update) | async-done | bytes 5242896 | tf_op jit(solution)/shard_map/all_gather | solution.py:99
  239.1 3.1 fusion.201
  242.4 5.3 %fusion.4 = (f32[2,1280]{1,0:T(2,128)S(1)}, f32[1024,1280,2]{1,0,2:T(8,128)}) fusion(pred[1280,1024]{0,1:T(8,128)(4,1)S(1)} %copy-done.13, bf16[1280,2,128]{0,2,1:T(8,128)(2,1)S(1)} %bitcast.478, bf16[1024,1,2,128]{0,3,2,1:T(8,128)(2,1)S(1)} %bitcast.469), kind=kOutput, calls=%fused_computation.27 | convolution fusion | flops 678950400 | bytes 12724224 | tf_op jit(solution)/shard_map/tkgd,skd->kgts/dot_general | solution.py:114
  247.6 5.2 %fusion.5 = (f32[2,1280]{1,0:T(2,128)S(1)}, f32[1024,1280,2]{1,0,2:T(8,128)}) fusion(pred[1280,1024]{0,1:T(8,128)(4,1)S(1)} %copy-done.11, bf16[1280,2,128]{0,2,1:T(8,128)(2,1)S(1)} %bitcast.479, bf16[1024,1,2,128]{0,3,2,1:T(8,128)(2,1)S(1)} %bitcast.467), kind=kOutput, calls=%fused_computation.28 | convolution fusion | flops 678950400 | bytes 12724224 | tf_op jit(solution)/shard_map/tkgd,skd->kgts/dot_general | solution.py:114
  252.8 5.1 %fusion.6 = (f32[2,1280]{1,0:T(2,128)S(1)}, f32[1024,1280,2]{1,0,2:T(8,128)}) fusion(pred[1280,1024]{0,1:T(8,128)(4,1)S(1)} %copy-done.9, bf16[1280,2,128]{0,2,1:T(8,128)(2,1)S(1)} %bitcast.480, bf16[1024,1,2,128]{0,3,2,1:T(8,128)(2,1)S(1)} %bitcast.465), kind=kOutput, calls=%fused_computation.29 | convolution fusion | flops 678950400 | bytes 12724224 | tf_op jit(solution)/shard_map/tkgd,skd->kgts/dot_general | solution.py:114
  258.0 5.2 %fusion.7 = (f32[2,1280]{1,0:T(2,128)S(1)}, f32[1024,1280,2]{1,0,2:T(8,128)}) fusion(pred[1280,1024]{0,1:T(8,128)(4,1)S(1)} %copy-done.7, bf16[1280,2,128]{0,2,1:T(8,128)(2,1)S(1)} %bitcast.481, bf16[1024,1,2,128]{0,3,2,1:T(8,128)(2,1)S(1)} %bitcast.463), kind=kOutput, calls=%fused_computation.30 | convolution fusion | flops 678950400 | bytes 12724224 | tf_op jit(solution)/shard_map/tkgd,skd->kgts/dot_general | solution.py:114
  263.2 5.3 %fusion.8 = (f32[2,1280]{1,0:T(2,128)S(1)}, f32[1024,1280,2]{1,0,2:T(8,128)}) fusion(pred[1280,1024]{0,1:T(8,128)(4,1)S(1)} %copy-done.5, bf16[1280,2,128]{0,2,1:T(8,128)(2,1)S(1)} %bitcast.482, bf16[1024,1,2,128]{0,3,2,1:T(8,128)(2,1)S(1)} %bitcast.461), kind=kOutput, calls=%fused_computation.31 | convolution fusion | flops 678950400 | bytes 12724224 | tf_op jit(solution)/shard_map/tkgd,skd->kgts/dot_general | solution.py:114
  268.5 5.2 %fusion.9 = (f32[2,1280]{1,0:T(2,128)S(1)}, f32[1024,1280,2]{1,0,2:T(8,128)}) fusion(pred[1280,1024]{0,1:T(8,128)(4,1)S(1)} %copy-done.4, bf16[1280,2,128]{0,2,1:T(8,128)(2,1)S(1)} %bitcast.483, bf16[1024,1,2,128]{0,3,2,1:T(8,128)(2,1)S(1)} %bitcast.459), kind=kOutput, calls=%fused_computation.32 | convolution fusion | flops 678950400 | bytes 12724224 | tf_op jit(solution)/shard_map/tkgd,skd->kgts/dot_general | solution.py:114
  273.7 5.3 %fusion.10 = (f32[2,1280]{1,0:T(2,128)S(1)}, f32[1024,1280,2]{1,0,2:T(8,128)}) fusion(pred[1280,1024]{0,1:T(8,128)(4,1)S(1)} %copy-done.3, bf16[1280,2,128]{0,2,1:T(8,128)(2,1)S(1)} %bitcast.484, bf16[1024,1,2,128]{0,3,2,1:T(8,128)(2,1)S(1)} %bitcast.457), kind=kOutput, calls=%fused_computation.33 | convolution fusion | flops 678950400 | bytes 12724224 | tf_op jit(solution)/shard_map/tkgd,skd->kgts/dot_general | solution.py:114
  279.1 5.1 %fusion.11 = (f32[2,1280]{1,0:T(2,128)S(1)}, f32[1024,1280,2]{1,0,2:T(8,128)}) fusion(pred[1280,1024]{0,1:T(8,128)(4,1)S(1)} %copy-done.2, bf16[1280,2,128]{0,2,1:T(8,128)(2,1)S(1)} %bitcast.485, bf16[1024,1,2,128]{0,3,2,1:T(8,128)(2,1)S(1)} %bitcast.455), kind=kOutput, calls=%fused_computation.34 | convolution fusion | flops 678950400 | bytes 12724224 | tf_op jit(solution)/shard_map/tkgd,skd->kgts/dot_general | solution.py:114
  284.2 2.3 fusion.12
  286.5 5.3 %fusion.3 = (f32[2,1280]{1,0:T(2,128)S(1)}, f32[1024,1280,2]{1,0,2:T(8,128)}) fusion(pred[1280,1024]{0,1:T(8,128)(4,1)S(1)} %copy-done.1, bf16[1280,2,128]{0,2,1:T(8,128)(2,1)S(1)} %bitcast.487, bf16[1024,1,2,128]{0,3,2,1:T(8,128)(2,1)S(1)} %bitcast.471), kind=kOutput, calls=%fused_computation.26 | convolution fusion | flops 678950400 | bytes 12724224 | tf_op jit(solution)/shard_map/tkgd,skd->kgts/dot_general | solution.py:114
  291.9 6.7 %fusion.13 = f32[2,1280]{1,0:T(2,128)S(1)} fusion(f32[1024,1280,2]{1,0,2:T(8,128)} %get-tuple-element.85, f32[2,1280]{1,0:T(2,128)S(1)} %get-tuple-element.64, pred[1280,1024]{0,1:T(8,128)(4,1)S(1)} %copy-done.1), kind=kLoop, calls=%fused_computation.36 | loop fusion | flops 13104640 | bytes 11816960 | tf_op jit(solution)/shard_map/reduce_sum | solution.py:123
  298.6 3.1 fusion.31
  301.8 6.7 %fusion.29 = f32[2,1280]{1,0:T(2,128)S(1)} fusion(f32[1024,1280,2]{1,0,2:T(8,128)} %get-tuple-element.69, f32[2,1280]{1,0:T(2,128)S(1)} %get-tuple-element.28, pred[1280,1024]{0,1:T(8,128)(4,1)S(1)} %copy-done.2), kind=kLoop, calls=%fused_computation.52 | loop fusion | flops 13104640 | bytes 11816960 | tf_op jit(solution)/shard_map/reduce_sum | solution.py:123
  308.5 6.7 %fusion.27 = f32[2,1280]{1,0:T(2,128)S(1)} fusion(f32[1024,1280,2]{1,0,2:T(8,128)} %get-tuple-element.71, f32[2,1280]{1,0:T(2,128)S(1)} %get-tuple-element.29, pred[1280,1024]{0,1:T(8,128)(4,1)S(1)} %copy-done.3), kind=kLoop, calls=%fused_computation.50 | loop fusion | flops 13104640 | bytes 11816960 | tf_op jit(solution)/shard_map/reduce_sum | solution.py:123
  315.3 6.7 %fusion.25 = f32[2,1280]{1,0:T(2,128)S(1)} fusion(f32[1024,1280,2]{1,0,2:T(8,128)} %get-tuple-element.73, f32[2,1280]{1,0:T(2,128)S(1)} %get-tuple-element.30, pred[1280,1024]{0,1:T(8,128)(4,1)S(1)} %copy-done.4), kind=kLoop, calls=%fused_computation.48 | loop fusion | flops 13104640 | bytes 11816960 | tf_op jit(solution)/shard_map/reduce_sum | solution.py:123
  322.0 7.0 %fusion.23 = f32[2,1280]{1,0:T(2,128)S(1)} fusion(f32[1024,1280,2]{1,0,2:T(8,128)} %get-tuple-element.75, f32[2,1280]{1,0:T(2,128)S(1)} %get-tuple-element.31, pred[1280,1024]{0,1:T(8,128)(4,1)} %get-tuple-element.57), kind=kLoop, calls=%fused_computation.46 | loop fusion | flops 13104640 | bytes 11816960 | tf_op jit(solution)/shard_map/reduce_sum | solution.py:123
  329.1 7.4 %fusion.21 = f32[2,1280]{1,0:T(2,128)S(1)} fusion(f32[1024,1280,2]{1,0,2:T(8,128)} %get-tuple-element.77, f32[2,1280]{1,0:T(2,128)S(1)} %get-tuple-element.32, pred[1280,1024]{0,1:T(8,128)(4,1)} %get-tuple-element.56), kind=kLoop, calls=%fused_computation.44 | loop fusion | flops 13104640 | bytes 11816960 | tf_op jit(solution)/shard_map/reduce_sum | solution.py:123
  336.5 7.0 %fusion.19 = f32[2,1280]{1,0:T(2,128)S(1)} fusion(f32[1024,1280,2]{1,0,2:T(8,128)} %get-tuple-element.79, f32[2,1280]{1,0:T(2,128)S(1)} %get-tuple-element.33, pred[1280,1024]{0,1:T(8,128)(4,1)} %get-tuple-element.55), kind=kLoop, calls=%fused_computation.42 | loop fusion | flops 13104640 | bytes 11816960 | tf_op jit(solution)/shard_map/reduce_sum | solution.py:123
  343.5 7.0 %fusion.17 = f32[2,1280]{1,0:T(2,128)S(1)} fusion(f32[1024,1280,2]{1,0,2:T(8,128)} %get-tuple-element.81, f32[2,1280]{1,0:T(2,128)S(1)} %get-tuple-element.34, pred[1280,1024]{0,1:T(8,128)(4,1)} %get-tuple-element.54), kind=kLoop, calls=%fused_computation.40 | loop fusion | flops 13104640 | bytes 11816960 | tf_op jit(solution)/shard_map/reduce_sum | solution.py:123
  350.6 7.0 %fusion.15 = f32[2,1280]{1,0:T(2,128)S(1)} fusion(f32[1024,1280,2]{1,0,2:T(8,128)} %get-tuple-element.83, f32[2,1280]{1,0:T(2,128)S(1)} %get-tuple-element.35, pred[1280,1024]{0,1:T(8,128)(4,1)} %get-tuple-element.53), kind=kLoop, calls=%fused_computation.38 | loop fusion | flops 13104640 | bytes 11816960 | tf_op jit(solution)/shard_map/reduce_sum | solution.py:123
  357.6 0.1 multiply_add_fusion
  357.7 8.9 %fusion.108 = f32[2,1280,128]{1,2,0:T(8,128)} fusion(f32[1024,1280,2]{1,0,2:T(8,128)} %get-tuple-element.85, f32[2,1280]{1,0:T(2,128)S(1)} %get-tuple-element.64, pred[1280,1024]{0,1:T(8,128)(4,1)S(1)} %copy-done.1, f32[2,1280]{1,0:T(2,128)S(1)} %get-tuple-element.26, f32[2,1280]{1,0:T(2,128)S(1)} %get-tuple-element.63, bf16[1024,1,2,128]{0,3,2,1:T(8,128)(2,1)} %bitcast.472), kind=kOutput, calls=%fused_computation.109 | convolution fusion | flops 684851200 | bytes 13400064 | tf_op jit(solution)/shard_map/kgts,skd->kgtd/dot_general | solution.py:124
  366.7 8.0 %fusion.111 = f32[2,1280,128]{1,2,0:T(8,128)} fusion(f32[2,1280,128]{1,2,0:T(8,128)} %fusion.108, f32[1024,1280,2]{1,0,2:T(8,128)} %get-tuple-element.83, f32[2,1280]{1,0:T(2,128)S(1)} %get-tuple-element.35, pred[1280,1024]{0,1:T(8,128)(4,1)} %get-tuple-element.53, f32[2,1280]{1,0:T(2,128)S(1)} %get-tuple-element.25, ...), kind=kOutput, calls=%fused_computation.110 | convolution fusion | flops 684851200 | bytes 14700544 | tf_op jit(solution)/shard_map/kgts,skd->kgtd/dot_general | solution.py:124
  374.8 5.8 %fusion.114 = f32[2,1280,128]{1,2,0:T(8,128)} fusion(f32[2,1280,128]{1,2,0:T(8,128)} %fusion.111, f32[1024,1280,2]{1,0,2:T(8,128)S(1)} %bitcast.446, f32[2,1280]{1,0:T(2,128)S(1)} %get-tuple-element.34, pred[1280,1024]{0,1:T(8,128)(4,1)S(1)} %copy-done.12, f32[2,1280]{1,0:T(2,128)S(1)} %get-tuple-element.24, bf16[1024,1,2,128]{0,3,2,1:T(8,128)(2,1)} %bitcast.468), kind=kOutput, calls=%fused_computation.111 | convolution fusion | flops 684851200 | bytes 14700544 | tf_op jit(solution)/shard_map/kgts,skd->kgtd/dot_general | solution.py:124
  380.6 7.9 %fusion.117 = f32[2,1280,128]{1,2,0:T(8,128)} fusion(f32[2,1280,128]{1,2,0:T(8,128)} %fusion.114, f32[1024,1280,2]{1,0,2:T(8,128)} %get-tuple-element.79, f32[2,1280]{1,0:T(2,128)S(1)} %get-tuple-element.33, pred[1280,1024]{0,1:T(8,128)(4,1)S(1)} %copy-done.10, f32[2,1280]{1,0:T(2,128)S(1)} %get-tuple-element.23, bf16[1024,1,2,128]{0,3,2,1:T(8,128)(2,1)S(1)} %bitcast.466), kind=kOutput, calls=%fused_computation.112 | convolution fusion | flops 684851200 | bytes 14700544 | tf_op jit(solution)/shard_map/kgts,skd->kgtd/dot_general | solution.py:124
  388.6 9.1 %fusion.120 = f32[2,1280,128]{1,2,0:T(8,128)} fusion(f32[2,1280,128]{1,2,0:T(8,128)} %fusion.117, f32[1024,1280,2]{1,0,2:T(8,128)} %get-tuple-element.77, f32[2,1280]{1,0:T(2,128)S(1)} %get-tuple-element.32, pred[1280,1024]{0,1:T(8,128)(4,1)S(1)} %copy-done.8, f32[2,1280]{1,0:T(2,128)S(1)} %get-tuple-element.22, bf16[1024,1,2,128]{0,3,2,1:T(8,128)(2,1)} %bitcast.464), kind=kOutput, calls=%fused_computation.113 | convolution fusion | flops 684851200 | bytes 14700544 | tf_op jit(solution)/shard_map/kgts,skd->kgtd/dot_general | solution.py:124
  397.7 5.8 %fusion.123 = f32[2,1280,128]{1,2,0:T(8,128)} fusion(f32[2,1280,128]{1,2,0:T(8,128)} %fusion.120, f32[1024,1280,2]{1,0,2:T(8,128)S(1)} %bitcast.444, f32[2,1280]{1,0:T(2,128)S(1)} %get-tuple-element.31, pred[1280,1024]{0,1:T(8,128)(4,1)S(1)} %copy-done.6, f32[2,1280]{1,0:T(2,128)S(1)} %get-tuple-element.21, bf16[1024,1,2,128]{0,3,2,1:T(8,128)(2,1)S(1)} %bitcast.462), kind=kOutput, calls=%fused_computation.114 | convolution fusion | flops 684851200 | bytes 14700544 | tf_op jit(solution)/shard_map/kgts,skd->kgtd/dot_general | solution.py:124
  403.6 6.9 %fusion.126 = f32[2,1280,128]{1,2,0:T(8,128)S(1)} fusion(f32[2,1280,128]{1,2,0:T(8,128)} %fusion.123, f32[1024,1280,2]{1,0,2:T(8,128)} %get-tuple-element.73, f32[2,1280]{1,0:T(2,128)S(1)} %get-tuple-element.30, pred[1280,1024]{0,1:T(8,128)(4,1)S(1)} %copy-done.4, f32[2,1280]{1,0:T(2,128)S(1)} %get-tuple-element.20, bf16[1024,1,2,128]{0,3,2,1:T(8,128)(2,1)S(1)} %bitcast.460), kind=kOutput, calls=%fused_computation.115 | convolution fusion | flops 684851200 | bytes 14700544 | tf_op jit(solution)/shard_map/kgts,skd->kgtd/dot_general | solution.py:124
  410.5 6.3 %fusion.129 = f32[2,1280,128]{1,2,0:T(8,128)S(1)} fusion(f32[2,1280,128]{1,2,0:T(8,128)S(1)} %fusion.126, f32[1024,1280,2]{1,0,2:T(8,128)} %get-tuple-element.71, f32[2,1280]{1,0:T(2,128)S(1)} %get-tuple-element.29, pred[1280,1024]{0,1:T(8,128)(4,1)S(1)} %copy-done.3, f32[2,1280]{1,0:T(2,128)S(1)} %get-tuple-element.19, ...), kind=kOutput, calls=%fused_computation.116 | convolution fusion | flops 684851200 | bytes 14700544 | tf_op jit(solution)/shard_map/kgts,skd->kgtd/dot_general | solution.py:124
  416.8 3.6 fusion.132
  420.5 3.7 fusion.144
  424.1 1.1 copy.189
  (122 shorter events, 1.0 us)
Async XLA Ops:
  10.3 61.4 %copy-start.29 = (bf16[256]{0:T(256)(128)(2,1)S(1)}, bf16[256]{0:T(256)(128)(2,1)}, u32[]{:S(2)}) copy-start(bf16[256]{0:T(256)(128)(2,1)} %param.9) | copy-start | bytes 1540
  12.3 46.4 %all-to-all-start = ((bf16[128,40,256]{2,1,0:T(8,128)(2,1)}), bf16[128,40,256]{2,1,0:T(8,128)(2,1)S(1)}, u32[]{:S(2)}, u32[]{:S(2)}) async-start(bf16[128,40,256]{2,1,0:T(8,128)(2,1)} %bitcast_select_fusion.10), calls=%async_computation | async-start | bytes 5242880 | tf_op jit(solution)/shard_map/all_to_all | solution.py:52
  23.8 156.2 %all-gather.4.cloned.1.call-start = ((), (), s32[]{:S(2)}) async-start(), calls=%async_computation.3 | async-start | bytes 11141120 | tf_op jit(solution)/shard_map/all_gather | solution.py:69
  67.7 40.9 %all-to-all-start.1 = ((bf16[256,16,128]{0,2,1:T(8,128)(2,1)}), bf16[256,16,128]{0,2,1:T(8,128)(2,1)S(1)}, u32[]{:S(2)}, u32[]{:S(2)}) async-start(bf16[256,16,128]{0,2,1:T(8,128)(2,1)} %bitcast.7), calls=%async_computation.1 | async-start | bytes 2097152 | tf_op jit(solution)/shard_map/all_to_all | solution.py:79
  108.5 109.4 %all-to-all-start.2 = ((bf16[256,16,256]{0,2,1:T(8,128)(2,1)}), bf16[256,16,256]{0,2,1:T(8,128)(2,1)S(1)}, u32[]{:S(2)}, u32[]{:S(2)}) async-start(bf16[256,16,256]{0,2,1:T(8,128)(2,1)} %bitcast.13), calls=%async_computation.2 | async-start | bytes 4194304 | tf_op jit(solution)/shard_map/all_to_all | solution.py:78
  112.4 126.7 %all-gather.6.cloned.1.call-start = ((), (), s32[]{:S(2)}) async-start(), calls=%async_computation.4 | async-start | bytes 5898240 | tf_op jit(solution)/shard_map/all_gather | solution.py:99
  180.0 7.0 %copy-start = (bf16[1280,4096]{1,0:T(8,128)(2,1)S(1)}, bf16[1280,4096]{1,0:T(8,128)(2,1)}, u32[]{:S(2)}) copy-start(bf16[1280,4096]{1,0:T(8,128)(2,1)} %all-gather.4.cloned.1.call-done) | copy-start | bytes 31457284
  191.9 7.8 %collective-permute-start = (bf16[1280,128]{0,1:T(8,128)(2,1)S(1)}, bf16[1280,128]{0,1:T(8,128)(2,1)S(1)}, u32[]{:S(2)}, u32[]{:S(2)}) collective-permute-start(bf16[1280,128]{0,1:T(8,128)(2,1)S(1)} %fusion.138), channel_id=1, source_target_pairs={{0,1},{1,0},{2,3},{3,2},{4,5},{5,4},{6,7},{7,6},{8,9},{9,8},{10,11... | collective-permute-start | bytes 983048 | tf_op jit(solution)/shard_map/ppermute | solution.py:15
  229.2 13.1 %copy-start.13 = (pred[1280,1024]{0,1:T(8,128)(4,1)S(1)}, pred[1280,1024]{0,1:T(8,128)(4,1)}, u32[]{:S(2)}) copy-start(pred[1280,1024]{0,1:T(8,128)(4,1)} %get-tuple-element.53) | copy-start | bytes 3932164
  239.1 3.2 copy-start.30
  242.2 10.6 %copy-start.25 = (bf16[1024,256]{0,1:T(8,128)(2,1)}, bf16[1024,256]{0,1:T(8,128)(2,1)S(1)}, u32[]{:S(2)}) copy-start(bf16[1024,256]{0,1:T(8,128)(2,1)S(1)} %get-tuple-element.49) | copy-start | bytes 1572868
  242.3 10.5 %copy-start.26 = (bf16[1024,256]{0,1:T(8,128)(2,1)}, bf16[1024,256]{0,1:T(8,128)(2,1)S(1)}, u32[]{:S(2)}) copy-start(bf16[1024,256]{0,1:T(8,128)(2,1)S(1)} %get-tuple-element.41) | copy-start | bytes 1572868
  242.3 10.5 %copy-start.23 = (bf16[1024,256]{0,1:T(8,128)(2,1)}, bf16[1024,256]{0,1:T(8,128)(2,1)S(1)}, u32[]{:S(2)}) copy-start(bf16[1024,256]{0,1:T(8,128)(2,1)S(1)} %get-tuple-element.48) | copy-start | bytes 1572868
  242.3 15.7 %copy-start.22 = (bf16[1024,256]{0,1:T(8,128)(2,1)}, bf16[1024,256]{0,1:T(8,128)(2,1)S(1)}, u32[]{:S(2)}) copy-start(bf16[1024,256]{0,1:T(8,128)(2,1)S(1)} %get-tuple-element.47) | copy-start | bytes 1572868
  242.3 20.9 %copy-start.20 = (bf16[1024,256]{0,1:T(8,128)(2,1)}, bf16[1024,256]{0,1:T(8,128)(2,1)S(1)}, u32[]{:S(2)}) copy-start(bf16[1024,256]{0,1:T(8,128)(2,1)S(1)} %get-tuple-element.46) | copy-start | bytes 1572868
  242.3 26.2 %copy-start.18 = (bf16[1024,256]{0,1:T(8,128)(2,1)}, bf16[1024,256]{0,1:T(8,128)(2,1)S(1)}, u32[]{:S(2)}) copy-start(bf16[1024,256]{0,1:T(8,128)(2,1)S(1)} %get-tuple-element.45) | copy-start | bytes 1572868
  242.3 31.4 %copy-start.16 = (bf16[1024,256]{0,1:T(8,128)(2,1)}, bf16[1024,256]{0,1:T(8,128)(2,1)S(1)}, u32[]{:S(2)}) copy-start(bf16[1024,256]{0,1:T(8,128)(2,1)S(1)} %get-tuple-element.44) | copy-start | bytes 1572868
  242.3 36.7 %copy-start.14 = (bf16[1024,256]{0,1:T(8,128)(2,1)}, bf16[1024,256]{0,1:T(8,128)(2,1)S(1)}, u32[]{:S(2)}) copy-start(bf16[1024,256]{0,1:T(8,128)(2,1)S(1)} %get-tuple-element.43) | copy-start | bytes 1572868
  242.3 44.2 %copy-start.28 = (bf16[1024,256]{0,1:T(8,128)(2,1)}, bf16[1024,256]{0,1:T(8,128)(2,1)S(1)}, u32[]{:S(2)}) copy-start(bf16[1024,256]{0,1:T(8,128)(2,1)S(1)} %get-tuple-element.50) | copy-start | bytes 1572868
  242.4 5.3 %copy-start.11 = (pred[1280,1024]{0,1:T(8,128)(4,1)S(1)}, pred[1280,1024]{0,1:T(8,128)(4,1)}, u32[]{:S(2)}) copy-start(pred[1280,1024]{0,1:T(8,128)(4,1)} %get-tuple-element.54) | copy-start | bytes 3932164
  247.6 5.2 %copy-start.9 = (pred[1280,1024]{0,1:T(8,128)(4,1)S(1)}, pred[1280,1024]{0,1:T(8,128)(4,1)}, u32[]{:S(2)}) copy-start(pred[1280,1024]{0,1:T(8,128)(4,1)} %get-tuple-element.55) | copy-start | bytes 3932164
  252.8 5.1 %copy-start.7 = (pred[1280,1024]{0,1:T(8,128)(4,1)S(1)}, pred[1280,1024]{0,1:T(8,128)(4,1)}, u32[]{:S(2)}) copy-start(pred[1280,1024]{0,1:T(8,128)(4,1)} %get-tuple-element.56) | copy-start | bytes 3932164
  258.0 5.3 %copy-start.5 = (pred[1280,1024]{0,1:T(8,128)(4,1)S(1)}, pred[1280,1024]{0,1:T(8,128)(4,1)}, u32[]{:S(2)}) copy-start(pred[1280,1024]{0,1:T(8,128)(4,1)} %get-tuple-element.57) | copy-start | bytes 3932164
  263.2 5.3 %copy-start.4 = (pred[1280,1024]{0,1:T(8,128)(4,1)S(1)}, pred[1280,1024]{0,1:T(8,128)(4,1)}, u32[]{:S(2)}) copy-start(pred[1280,1024]{0,1:T(8,128)(4,1)} %get-tuple-element.58) | copy-start | bytes 3932164
  268.5 5.2 %copy-start.3 = (pred[1280,1024]{0,1:T(8,128)(4,1)S(1)}, pred[1280,1024]{0,1:T(8,128)(4,1)}, u32[]{:S(2)}) copy-start(pred[1280,1024]{0,1:T(8,128)(4,1)} %get-tuple-element.59) | copy-start | bytes 3932164
  273.7 5.3 %copy-start.2 = (pred[1280,1024]{0,1:T(8,128)(4,1)S(1)}, pred[1280,1024]{0,1:T(8,128)(4,1)}, u32[]{:S(2)}) copy-start(pred[1280,1024]{0,1:T(8,128)(4,1)} %get-tuple-element.60) | copy-start | bytes 3932164
  284.2 2.3 copy-start.1
  357.7 9.0 %copy-start.27 = (bf16[1024,256]{0,1:T(8,128)(2,1)S(1)}, bf16[1024,256]{0,1:T(8,128)(2,1)}, u32[]{:S(2)}) copy-start(bf16[1024,256]{0,1:T(8,128)(2,1)} %copy-done.26) | copy-start | bytes 1572868
  357.7 17.0 %slice-start.6 = ((s8[10485760]{0:T(1024)(128)(4,1)}), s8[4194304]{0:T(1024)(128)(4,1)S(1)}, s32[]{:S(2)}) async-start(s8[10485760]{0:T(1024)(128)(4,1)} %bitcast.445), calls=%async_computation.11 | async-start | bytes 8388608
  357.7 17.0 %slice-start.7 = ((s8[10485760]{0:T(1024)(128)(4,1)}), s8[4194304]{0:T(1024)(128)(4,1)S(1)}, s32[]{:S(2)}) async-start(s8[10485760]{0:T(1024)(128)(4,1)} %bitcast.445), calls=%async_computation.12 | async-start | bytes 8388608
  366.7 8.1 %slice-start.8 = ((s8[10485760]{0:T(1024)(128)(4,1)}), s8[2097152]{0:T(1024)(128)(4,1)S(1)}, s32[]{:S(2)}) async-start(s8[10485760]{0:T(1024)(128)(4,1)} %bitcast.445), calls=%async_computation.13 | async-start | bytes 4194304
  366.7 8.1 %copy-start.12 = (pred[1280,1024]{0,1:T(8,128)(4,1)S(1)}, pred[1280,1024]{0,1:T(8,128)(4,1)}, u32[]{:S(2)}) copy-start(pred[1280,1024]{0,1:T(8,128)(4,1)} %get-tuple-element.54) | copy-start | bytes 3932164
  374.8 5.8 %copy-start.10 = (pred[1280,1024]{0,1:T(8,128)(4,1)S(1)}, pred[1280,1024]{0,1:T(8,128)(4,1)}, u32[]{:S(2)}) copy-start(pred[1280,1024]{0,1:T(8,128)(4,1)} %get-tuple-element.55) | copy-start | bytes 3932164
  374.8 5.8 %copy-start.24 = (bf16[1024,256]{0,1:T(8,128)(2,1)S(1)}, bf16[1024,256]{0,1:T(8,128)(2,1)}, u32[]{:S(2)}) copy-start(bf16[1024,256]{0,1:T(8,128)(2,1)} %copy-done.23) | copy-start | bytes 1572868
  380.6 7.9 %copy-start.8 = (pred[1280,1024]{0,1:T(8,128)(4,1)S(1)}, pred[1280,1024]{0,1:T(8,128)(4,1)}, u32[]{:S(2)}) copy-start(pred[1280,1024]{0,1:T(8,128)(4,1)} %get-tuple-element.56) | copy-start | bytes 3932164
  380.6 17.0 %slice-start.3 = ((s8[10485760]{0:T(1024)(128)(4,1)}), s8[4194304]{0:T(1024)(128)(4,1)S(1)}, s32[]{:S(2)}) async-start(s8[10485760]{0:T(1024)(128)(4,1)} %bitcast.443), calls=%async_computation.8 | async-start | bytes 8388608
  380.6 17.0 %slice-start.4 = ((s8[10485760]{0:T(1024)(128)(4,1)}), s8[4194304]{0:T(1024)(128)(4,1)S(1)}, s32[]{:S(2)}) async-start(s8[10485760]{0:T(1024)(128)(4,1)} %bitcast.443), calls=%async_computation.9 | async-start | bytes 8388608
  388.5 9.1 %slice-start.5 = ((s8[10485760]{0:T(1024)(128)(4,1)}), s8[2097152]{0:T(1024)(128)(4,1)S(1)}, s32[]{:S(2)}) async-start(s8[10485760]{0:T(1024)(128)(4,1)} %bitcast.443), calls=%async_computation.10 | async-start | bytes 4194304
  388.5 9.1 %copy-start.6 = (pred[1280,1024]{0,1:T(8,128)(4,1)S(1)}, pred[1280,1024]{0,1:T(8,128)(4,1)}, u32[]{:S(2)}) copy-start(pred[1280,1024]{0,1:T(8,128)(4,1)} %get-tuple-element.57) | copy-start | bytes 3932164
  388.5 9.1 %copy-start.21 = (bf16[1024,256]{0,1:T(8,128)(2,1)S(1)}, bf16[1024,256]{0,1:T(8,128)(2,1)}, u32[]{:S(2)}) copy-start(bf16[1024,256]{0,1:T(8,128)(2,1)} %copy-done.20) | copy-start | bytes 1572868
  397.7 5.8 %copy-start.19 = (bf16[1024,256]{0,1:T(8,128)(2,1)S(1)}, bf16[1024,256]{0,1:T(8,128)(2,1)}, u32[]{:S(2)}) copy-start(bf16[1024,256]{0,1:T(8,128)(2,1)} %copy-done.18) | copy-start | bytes 1572868
  403.5 6.9 %copy-start.17 = (bf16[1024,256]{0,1:T(8,128)(2,1)S(1)}, bf16[1024,256]{0,1:T(8,128)(2,1)}, u32[]{:S(2)}) copy-start(bf16[1024,256]{0,1:T(8,128)(2,1)} %copy-done.16) | copy-start | bytes 1572868
  403.5 13.2 %slice-start = ((s8[10485760]{0:T(1024)(128)(4,1)}), s8[4194304]{0:T(1024)(128)(4,1)S(1)}, s32[]{:S(2)}) async-start(s8[10485760]{0:T(1024)(128)(4,1)} %bitcast.441), calls=%async_computation.5 | async-start | bytes 8388608
  403.5 13.2 %slice-start.1 = ((s8[10485760]{0:T(1024)(128)(4,1)}), s8[4194304]{0:T(1024)(128)(4,1)S(1)}, s32[]{:S(2)}) async-start(s8[10485760]{0:T(1024)(128)(4,1)} %bitcast.441), calls=%async_computation.6 | async-start | bytes 8388608
  410.5 6.3 %slice-start.2 = ((s8[10485760]{0:T(1024)(128)(4,1)}), s8[2097152]{0:T(1024)(128)(4,1)S(1)}, s32[]{:S(2)}) async-start(s8[10485760]{0:T(1024)(128)(4,1)} %bitcast.441), calls=%async_computation.7 | async-start | bytes 4194304
  410.5 6.3 %copy-start.15 = (bf16[1024,256]{0,1:T(8,128)(2,1)S(1)}, bf16[1024,256]{0,1:T(8,128)(2,1)}, u32[]{:S(2)}) copy-start(bf16[1024,256]{0,1:T(8,128)(2,1)} %copy-done.14) | copy-start | bytes 1572868
Sparse Core Ops, SparseCore 0:
  65.5 114.4 all-gather.3
  200.7 38.3 all-gather.5
where the time goes:
time: 440 us; the launch traced here: 432 us
  matrix products  129 us (29%)
  waiting for transfers between devices  117 us (27%)
  other arithmetic  96.6 us (22%)
  blocking collectives  32.7 us (7%)
  local copies, waits for them, and re-layouts  21.9 us (5%)
  starting transfers between devices  20.9 us (5%)
  between operations  14.4 us (3%)
    all_gather x1, waiting for transfers between devices, per_device(): lax.all_gather(stream, 'enc', axis=1, tiled=True)  66.1 us
    dot_general x10, matrix products, per_device(): jnp.einsum('kgts,skd->kgtd', weights.astype(jnp.bfloat16), key_block[:, :...  66.1 us
    reduce_sum x10, other arithmetic, per_device(): new_sum = update_run_sum * rescale + jnp.sum(weights, axis=-1)  65.7 us
    dot_general x10, matrix products, per_device(): jnp.einsum('tkgd,skd->kgts', grouped, key_block[:, :, 0, :], preferred_el...  49.3 us
    all_to_all x1, waiting for transfers between devices, per_device(): lax.all_to_all(outgoing.reshape(seq_count * enc_count, vis_rows, feature_...  34.6 us
    all_gather x1, blocking collectives, per_device(): lax.all_gather(gain, 'enc', axis=0, tiled=True)  32.7 us
    or x2, other arithmetic, per_device(): (key_pos[None, :] <= positions[:, None]) | (query_span[:, None] == key_sp...  17.2 us
    all_to_all x1, starting transfers between devices, per_device(): lax.all_to_all(outgoing.reshape(seq_count * enc_count, vis_rows, feature_...  11.5 us
  transfers between devices with their start and end apart: 6, of which 4 were waited for; matrix products, arithmetic and copies ran while one was open for 11% of the time, Pallas kernels for 0%

commit v1 on v0

v1 whole, which is shorter than its diff:
```python
import functools
import math

import jax
import jax.numpy as jnp
from jax import lax
from jax.experimental import pallas as pl
from jax.experimental.pallas import tpu as pltpu
from jax.sharding import PartitionSpec as P

HD = 128
EPS = 1e-05
WINDOW = 16
NEG = -1e30
SAFE = 64.0
VMEM = pltpu.VMEM


def layout(image_count, text_gap):
    offsets = jnp.cumsum(image_count) - image_count
    starts = jnp.cumsum(text_gap[:-1]) + offsets
    return (offsets, starts)


def assemble_kernel(tile, index_ref, text_ref, arrived_ref, out_ref):
    slots = arrived_ref.shape[0]

    @pl.loop(0, text_ref.shape[0] // tile)
    def _(step):
        rows = pl.ds(pl.multiple_of(step * tile, tile), tile)
        index = index_ref[rows, :]
        lanes = lax.broadcasted_iota(jnp.int32, (tile, slots), 1)
        chosen = jnp.where(lanes == index, 1.0, 0.0).astype(jnp.bfloat16)
        picked = jnp.dot(chosen, arrived_ref[...], preferred_element_type=jnp.float32)
        out_ref[rows, :] = jnp.where(index >= 0, picked.astype(jnp.bfloat16), text_ref[rows, :])


def assemble(index, text, arrived):
    return pl.pallas_call(
        functools.partial(assemble_kernel, 128),
        out_shape=jax.ShapeDtypeStruct(text.shape, text.dtype),
        in_specs=[pl.BlockSpec(memory_space=VMEM)] * 3,
        out_specs=pl.BlockSpec(memory_space=VMEM),
    )(index, text, arrived)


def attention_kernel(bq, bk, sbq, sbk, off_ref, q_ref, kv_ref, lim_ref, o_ref, acc, den, top):
    heads = q_ref.shape[1] // HD
    rows_all, keys_all = q_ref.shape[0], kv_ref.shape[0]
    q0 = off_ref[0]

    def query_norm(step, best):
        block = q_ref[pl.ds(pl.multiple_of(step * 128, 128), 128), :].astype(jnp.float32)
        square = block * block
        for head in range(heads):
            norm = jnp.sum(square[:, head * HD : (head + 1) * HD], axis=1, keepdims=True)
            best = jnp.maximum(best, norm)
        return best

    def key_norm(step, best):
        block = kv_ref[pl.ds(pl.multiple_of(step * 128, 128), 128), :HD].astype(jnp.float32)
        return jnp.maximum(best, jnp.sum(block * block, axis=1, keepdims=True))

    zero = jnp.zeros((128, 1), jnp.float32)
    largest_query = jnp.max(lax.fori_loop(0, rows_all // 128, query_norm, zero))
    largest_key = jnp.max(lax.fori_loop(0, keys_all // 128, key_norm, zero))
    safe = largest_query * largest_key < SAFE * SAFE

    def scores(row, head, size, key, count, masked):
        q = q_ref[pl.ds(row, size), head * HD : (head + 1) * HD]
        s = lax.dot_general(
            q,
            kv_ref[pl.ds(key, count), :HD],
            (((1,), (1,)), ((), ())),
            preferred_element_type=jnp.float32,
        )
        if masked:
            at = key + lax.broadcasted_iota(jnp.int32, (size, count), 1)
            s = jnp.where(at <= lim_ref[pl.ds(row, size), :], s, NEG)
        return s

    def lane_sums(p):
        total = p[:, :HD]
        for part in range(1, p.shape[1] // HD):
            total = total + p[:, part * HD : (part + 1) * HD]
        return total

    def tiles(size, count, begin, step, end):
        @pl.loop(0, rows_all // size)
        def _(tile):
            row = pl.multiple_of(tile * size, size)
            begin()
            first = q0 + row
            whole = first // count
            last = jnp.minimum(pl.cdiv(first + size + 255, count), keys_all // count)

            @pl.loop(0, whole)
            def _(j):
                step(row, pl.multiple_of(j * count, count), False)

            @pl.loop(whole, last)
            def _(j):
                step(row, pl.multiple_of(j * count, count), True)

            end(row)

    @pl.when(safe)
    def _():
        def begin():
            acc[...] = jnp.zeros_like(acc)
            den[...] = jnp.zeros_like(den)

        def step(row, key, masked):
            values = kv_ref[pl.ds(key, bk), HD:]
            for head in range(heads):
                p = jnp.exp2(scores(row, head, bq, key, bk, masked))
                acc[head] += jnp.dot(
                    p.astype(jnp.bfloat16), values, preferred_element_type=jnp.float32
                )
                den[head] += lane_sums(p)

        def end(row):
            for head in range(heads):
                result = acc[head] / jnp.sum(den[head], axis=1, keepdims=True)
                o_ref[pl.ds(row, bq), head * HD : (head + 1) * HD] = result.astype(jnp.bfloat16)

        tiles(bq, bk, begin, step, end)

    @pl.when(jnp.logical_not(safe))
    def _():
        part = pl.ds(0, sbq)

        def begin():
            acc[...] = jnp.zeros_like(acc)
            den[...] = jnp.zeros_like(den)
            top[...] = jnp.full_like(top, NEG)

        def step(row, key, masked):
            values = kv_ref[pl.ds(key, sbk), HD:]
            for head in range(heads):
                s = scores(row, head, sbq, key, sbk, masked)
                old = top[head]
                new = jnp.maximum(old, jnp.max(s, axis=1, keepdims=True))
                top[head] = new
                p = jnp.exp2(s - new)
                shrink = jnp.exp2(old - new)
                acc[head, part] = acc[head, part] * shrink + jnp.dot(
                    p.astype(jnp.bfloat16), values, preferred_element_type=jnp.float32
                )
                den[head, part] = den[head, part] * shrink + lane_sums(p)

        def end(row):
            for head in range(heads):
                result = acc[head, part] / jnp.sum(den[head, part], axis=1, keepdims=True)
                o_ref[pl.ds(row, sbq), head * HD : (head + 1) * HD] = result.astype(jnp.bfloat16)

        tiles(sbq, sbk, begin, step, end)


def attention(q0, query, keyval, lim):
    rows, width = query.shape
    heads = width // HD
    bq, bk, sbq, sbk = rows // 2, 1024, 128, 512
    flops = 4 * rows * keyval.shape[0] * width
    return pl.pallas_call(
        functools.partial(attention_kernel, bq, bk, sbq, sbk),
        out_shape=jax.ShapeDtypeStruct(query.shape, jnp.bfloat16),
        in_specs=[pl.BlockSpec(memory_space=pltpu.SMEM)] + [pl.BlockSpec(memory_space=VMEM)] * 3,
        out_specs=pl.BlockSpec(memory_space=VMEM),
        scratch_shapes=[
            VMEM((heads, bq, HD), jnp.float32),
            VMEM((heads, bq, HD), jnp.float32),
            VMEM((heads, sbq, 1), jnp.float32),
        ],
        compiler_params=pltpu.CompilerParams(vmem_limit_bytes=56 << 20),
        cost_estimate=pl.CostEstimate(
            flops=flops, bytes_accessed=keyval.size * 2, transcendentals=rows * keyval.shape[0]
        ),
    )(q0, query, keyval, lim)


def per_device(text, visual, gain, w_query, w_keyval, image_count, text_gap):
    rows, features = text.shape
    vis_rows = visual.shape[0]
    seq_count, enc_count = lax.axis_size("seq"), lax.axis_size("enc")
    seq_index, enc_index = lax.axis_index("seq"), lax.axis_index("enc")
    device_total = seq_count * enc_count
    side = math.isqrt(enc_count)
    near = [[z * side + x for x in range(side)] for z in range(side)]
    far = [[z * side + x for z in range(side)] for x in range(side)]

    w = jnp.concatenate(
        (
            w_query.reshape(features, side, side, -1),
            w_keyval.reshape(features, side, side, -1),
        ),
        axis=3,
    )
    columns = w.shape[3]
    q_columns = w_query.shape[1] // enc_count
    w = (w.astype(jnp.float32) * gain.astype(jnp.float32)[:, None, None, None]).astype(jnp.bfloat16)
    w = jnp.transpose(w, (2, 0, 1, 3)).reshape(side, features, side * columns)
    w = lax.all_to_all(w, "enc", split_axis=0, concat_axis=0, axis_index_groups=near, tiled=True)
    w = w.reshape(side * features, side * columns)

    offsets, starts = layout(image_count, text_gap)
    ends = starts + image_count
    edges = jnp.arange(seq_count, dtype=jnp.int32) * rows
    before = jnp.sum(
        jnp.clip(edges[:, None] - starts[None, :], 0, image_count[None, :]), axis=1
    ).astype(jnp.int32)
    first_row = jnp.minimum(before // device_total, vis_rows - WINDOW)
    pieces = jnp.stack(
        [lax.dynamic_slice_in_dim(visual, first_row[s], WINDOW, 0) for s in range(seq_count)]
    )
    pieces = pieces.reshape(seq_count, WINDOW, enc_count, features)
    pieces = jnp.transpose(pieces, (0, 2, 1, 3)).reshape(device_total, WINDOW, features)
    arrived = lax.all_to_all(pieces, ("seq", "enc"), split_axis=0, concat_axis=0, tiled=True)
    arrived = arrived.reshape(device_total * WINDOW, features)

    positions = seq_index * rows + jnp.arange(rows, dtype=jnp.int32)
    inside = (positions[:, None] >= starts[None, :]) & (positions[:, None] < ends[None, :])
    is_visual = jnp.any(inside, axis=1)
    token = jnp.sum(jnp.where(inside, (offsets - starts)[None, :], 0), axis=1) + positions
    slot = token % device_total * WINDOW + token // device_total - first_row[seq_index]
    index = jnp.where(is_visual, slot, -1).astype(jnp.int32)
    last_key = jnp.maximum(
        jnp.sum(jnp.where(inside, ends[None, :], 0), axis=1) - 1, positions
    ).astype(jnp.int32)
    stream = assemble(index[:, None], text, arrived)

    widened = stream.astype(jnp.float32)
    square = lax.psum(jnp.sum(widened * widened, axis=1), "enc")
    scale = lax.rsqrt(square / (features * enc_count) + EPS)[:, None]
    gathered = lax.all_gather(stream, "enc", axis=1, axis_index_groups=near, tiled=True)
    partial = jnp.dot(gathered, w, preferred_element_type=jnp.float32).astype(jnp.bfloat16)
    summed = lax.psum_scatter(
        partial, "enc", scatter_dimension=1, axis_index_groups=far, tiled=True
    ).astype(jnp.float32)
    query = (summed[:, :q_columns] * (scale * (math.log2(math.e) / HD**0.5))).astype(jnp.bfloat16)
    own = (summed[:, q_columns:] * scale).astype(jnp.bfloat16)
    partner = lax.ppermute(own, "enc", [(i, i ^ 1) for i in range(enc_count)])
    holds_keys = enc_index % 2 == 0
    keyval = jnp.concatenate(
        (jnp.where(holds_keys, own, partner), jnp.where(holds_keys, partner, own)), axis=1
    )
    keyval = lax.all_gather(keyval, "seq", axis=0, tiled=True)
    q0 = (seq_index * rows).astype(jnp.int32).reshape(1)
    return attention(q0, query, keyval, last_key[:, None])


def solution(mesh):
    in_specs = (
        P("seq", "enc"),
        P(("seq", "enc"), None),
        P("enc"),
        P("enc", None),
        P("enc", None),
        P(),
        P(),
    )
    out_specs = P("seq", "enc")
    return jax.shard_map(
        per_device, mesh=mesh, in_specs=in_specs, out_specs=out_specs, check_vma=False
    )
```

time: 440 us -> 417 us (0.948)
  the two profiles are of different devices: /device:TPU:1 before, /device:TPU:25 now
where the time goes in v1:
time: 417 us; the launch traced here: 416 us
  Pallas kernels  178 us (43%)
  blocking collectives  89 us (21%)
  waiting for transfers between devices  68.6 us (16%)
  between operations  28.3 us (7%)
  local copies, waits for them, and re-layouts  23.3 us (6%)
  starting transfers between devices  10.8 us (3%)
  other arithmetic  9.16 us (2%)
  matrix products  8.79 us (2%)
    pallas_call x1, Pallas kernels, attention(): pl.pallas_call(functools.partial(attention_kernel, bq, bk, sbq, sbk), out...  172 us
    all_to_all x1, blocking collectives, per_device(): lax.all_to_all(w, 'enc', split_axis=0, concat_axis=0, axis_index_groups=n...  59.2 us
    all_gather x1, waiting for transfers between devices, per_device(): keyval = lax.all_gather(keyval, 'seq', axis=0, tiled=True)  32.6 us
    psum x1, blocking collectives, per_device(): square = lax.psum(jnp.sum(widened * widened, axis=1), 'enc')  29.8 us
    unnamed x25, local copies, waits for them, and re-layouts  14.8 us
    all_to_all x1, waiting for transfers between devices, per_device(): lax.all_to_all(pieces, ('seq', 'enc'), split_axis=0, concat_axis=0, tiled...  14.7 us
    unnamed x4, waiting for transfers between devices  12.6 us
    all_to_all x1, starting transfers between devices, per_device(): lax.all_to_all(pieces, ('seq', 'enc'), split_axis=0, concat_axis=0, tiled...  10.6 us
  transfers between devices with their start and end apart: 5, of which 4 were waited for; matrix products, arithmetic and copies ran while one was open for 3% of the time, Pallas kernels for 0%

profile of v1, /device:TPU:25, one launch (start us, length us, event | category | flops | bytes accessed | tf_op | source)
XLA Modules:
  0.0 416.2 jit_solution(2499701638185626652)
XLA Ops:
  6.5 0.7 slice_bitcast_fusion
  7.2 0.1 copy.35
  7.3 0.1 reduce-window.16
  7.3 0.1 reduce
  7.5 0.7 copy.36
  8.2 0.1 reduce-window.17
  8.3 0.1 reduce.1
  8.4 0.7 fusion.14
  9.0 0.8 minimum_reduce_fusion
  9.9 0.7 fusion.15
  25.4 1.9 constant_dynamic-slice_fusion
  27.8 1.4 copy.39
  29.1 10.6 %all-to-all-start = ((bf16[128,16,256]{2,1,0:T(8,128)(2,1)}), bf16[128,16,256]{2,1,0:T(8,128)(2,1)S(1)}, u32[]{:S(2)}, u32[]{:S(2)}) async-start(bf16[128,16,256]{2,1,0:T(8,128)(2,1)} %bitcast.13), calls=%async_computation | async-start | bytes 2097152 | tf_op jit(solution)/shard_map/all_to_all | solution.py:218
  39.7 0.0 all-gather.3.cloned.1.call-start
  39.8 0.1 fusion.12
  39.9 0.1 select_reduce_fusion
  40.0 2.5 fusion.5.index_ref
  42.5 14.7 %all-to-all-done = bf16[128,16,256]{2,1,0:T(8,128)(2,1)S(1)} async-done(((bf16[128,16,256]{2,1,0:T(8,128)(2,1)}), bf16[128,16,256]{2,1,0:T(8,128)(2,1)S(1)}, u32[]{:S(2)}, u32[]{:S(2)}) %all-to-all-start) | async-done | bytes 1048608 | tf_op jit(solution)/shard_map/all_to_all | solution.py:218
  57.3 0.0 copy-start.1
  57.3 1.0 copy-done.1
  58.2 6.3 %shard_map.73 = bf16[1280,256]{1,0:T(8,128)(2,1)} custom-call(s32[1280,1]{1,0:T(8,128)} %fusion.5.index_ref, bf16[1280,256]{1,0:T(8,128)(2,1)} %text_ref.1, bf16[2048,256]{1,0:T(8,128)(2,1)} %bitcast.69), custom_call_target="tpu_custom_call" | custom-call | tf_op jit(solution)/shard_map/pallas_call | solution.py:39
  64.6 0.0 all-gather.3.cloned.1.call-update
  64.6 0.0 copy-start.2
  64.6 0.0 reduce-scatter.4.cloned.1.call-start
  64.7 3.3 copy.40
  67.9 1.5 copy.41
  69.4 0.0 copy-done.2
  69.5 0.6 fusion
  70.1 0.2 copy.42
  70.3 59.2 %all_to_all.10 = bf16[4,256,1536]{1,2,0:T(8,128)(2,1)S(1)} all-to-all(bf16[4,256,1536]{1,2,0:T(8,128)(2,1)S(1)} %bitcast.67), channel_id=1, replica_groups={{0,1,2,3},{4,5,6,7},{8,9,10,11},{12,13,14,15},{16,17,18,19},{20,21,22,2..., dimensions={0} | all-to-all | bytes 6291456 | tf_op jit(solution)/shard_map/all_to_all | solution.py:203
  129.5 2.8 copy.43
  132.3 0.0 all-gather.3.cloned.1.call-done
  132.3 8.8 %convolution_convert_fusion = bf16[1280,1536]{1,0:T(8,128)(2,1)} fusion(bf16[1280,1024]{1,0:T(8,128)(2,1)} %all-gather.3.cloned.1.call-done, bf16[1024,1536]{1,0:T(8,128)(2,1)} %bitcast.71), kind=kOutput, calls=%fused_computation | convolution fusion | flops 4028497920 | bytes 9699328 | tf_op jit(solution)/shard_map/dot_general | solution.py:236
  141.1 6.2 %copy.45 = bf16[1280,1536]{0,1:T(8,128)(2,1)} copy(bf16[1280,1536]{1,0:T(8,128)(2,1)} %convolution_convert_fusion) | data formatting | bytes 7864320
  147.3 0.0 copy-start
  147.3 0.0 reduce-scatter.4.cloned.1.call-update
  147.3 0.0 all-gather.5.cloned.1.call-start
  147.4 1.0 copy-done
  148.4 0.2 multiply_reduce_fusion
  148.6 29.8 %psum.7 = f32[1280]{0:T(1024)S(1)} all-reduce(f32[1280]{0:T(1024)S(1)} %multiply_reduce_fusion), channel_id=1, replica_groups=mesh['seq'=8,'enc'=16] {'enc'}, use_global_device_ids=true, to_apply=%region_7.8 | all-reduce | flops 1280 | bytes 10240 | tf_op jit(solution)/shard_map/psum | solution.py:233
  178.4 12.6 %reduce-scatter.4.cloned.1.call-done = bf16[384,1280]{1,0:T(8,128)(2,1)} async-done(((bf16[1536,1280]{1,0:T(8,128)(2,1)}), bf16[384,1280]{1,0:T(8,128)(2,1)}) %reduce-scatter.4.cloned.1.call-update) | async-done | bytes 983056
  191.0 1.6 copy.46
  192.6 0.1 convert_element_type.28
  192.7 0.2 fusion.6
  192.9 0.1 collective-permute-start
  193.0 8.6 %collective-permute-done = bf16[1280,128]{1,0:T(8,128)(2,1)S(1)} collective-permute-done((bf16[1280,128]{1,0:T(8,128)(2,1)S(1)}, bf16[1280,128]{1,0:T(8,128)(2,1)S(1)}, u32[]{:S(2)}, u32[]{:S(2)}) %collective-permute-start) | collective-permute-done | bytes 327712 | tf_op jit(solution)/shard_map/ppermute | solution.py:242
  201.6 0.2 broadcast_select_fusion.1
  201.9 0.9 pad_maximum_fusion
  202.8 0.0 all-gather.5.cloned.1.call-update
  202.8 1.1 reshape_maximum_fusion.lim_ref
  203.9 1.1 fusion.1.q_ref
  205.0 32.6 %all-gather.5.cloned.1.call-done.kv_ref = bf16[10240,256]{1,0:T(8,128)(2,1)} async-done(((bf16[1280,256]{1,0:T(8,128)(2,1)}), bf16[10240,256]{1,0:T(8,128)(2,1)}) %all-gather.5.cloned.1.call-update) | async-done | bytes 5242896 | tf_op jit(solution)/shard_map/all_gather | solution.py:247
  237.6 172.0 %shard_map.74 = bf16[1280,256]{1,0:T(8,128)(2,1)} custom-call(s32[1]{0:T(128)} %bitcast.off_ref, bf16[1280,256]{1,0:T(8,128)(2,1)} %fusion.1.q_ref, bf16[10240,256]{1,0:T(8,128)(2,1)} %all-gather.5.cloned.1.call-done.kv_ref, s32[1280,1]{1,0:T(8,128)} %reshape_maximum_fusion.lim_ref), custom_call_target="tpu_custom_call" | custom-call | flops 13421772800 | bytes 5242880 | tf_op jit(solution)/shard_map/pallas_call | solution.py:165
  (22 shorter events, 0.3 us)
Async XLA Ops:
  29.1 28.1 %all-to-all-start = ((bf16[128,16,256]{2,1,0:T(8,128)(2,1)}), bf16[128,16,256]{2,1,0:T(8,128)(2,1)S(1)}, u32[]{:S(2)}, u32[]{:S(2)}) async-start(bf16[128,16,256]{2,1,0:T(8,128)(2,1)} %bitcast.13), calls=%async_computation | async-start | bytes 2097152 | tf_op jit(solution)/shard_map/all_to_all | solution.py:218
  39.7 92.6 %all-gather.3.cloned.1.call-start = ((), (), s32[]{:S(2)}) async-start(), calls=%async_computation.3 | async-start | bytes 3276800 | tf_op jit(solution)/shard_map/all_gather | solution.py:235
  57.3 1.0 copy-start.1
  64.6 4.8 %copy-start.2 = (bf16[256]{0:T(256)(128)(2,1)S(1)}, bf16[256]{0:T(256)(128)(2,1)}, u32[]{:S(2)}) copy-start(bf16[256]{0:T(256)(128)(2,1)} %param.9) | copy-start | bytes 1540
  64.6 126.4 %reduce-scatter.4.cloned.1.call-start = ((), (), s32[]{:S(2)}) async-start(), calls=%async_computation.5 | async-start | bytes 4915200
  147.3 1.1 copy-start
  147.3 90.3 %all-gather.5.cloned.1.call-start = ((), (), s32[]{:S(2)}) async-start(), calls=%async_computation.4 | async-start | bytes 5898240 | tf_op jit(solution)/shard_map/all_gather | solution.py:247
  192.9 8.7 %collective-permute-start = (bf16[1280,128]{1,0:T(8,128)(2,1)S(1)}, bf16[1280,128]{1,0:T(8,128)(2,1)S(1)}, u32[]{:S(2)}, u32[]{:S(2)}) collective-permute-start(bf16[1280,128]{1,0:T(8,128)(2,1)S(1)} %fusion.6), channel_id=1, source_target_pairs={{0,1},{1,0},{2,3},{3,2},{4,5},{5,4},{6,7},{7,6},{8,9},{9,8},{10,11... | collective-permute-start | bytes 983048 | tf_op jit(solution)/shard_map/ppermute | solution.py:242
Sparse Core Ops, SparseCore 0:
  64.7 65.5 all-gather.2
  147.5 43.4 reduce-scatter.3
  202.9 34.6 all-gather.4

commit v2 on v1

v2 whole, which is shorter than its diff:
```python
import functools
import math

import jax
import jax.numpy as jnp
from jax import lax
from jax.experimental import pallas as pl
from jax.experimental.pallas import tpu as pltpu
from jax.sharding import PartitionSpec as P

HD = 128
EPS = 1e-05
CHUNK = 128
MESH = pl.DeviceIdType.MESH
NEG = -1e30
SAFE = 64.0
VMEM = pltpu.VMEM


def spread(row):
    return jnp.broadcast_to(row, (HD, HD)).T


def project_kernel(
    side, count_ref, gap_ref, text_ref, visual_ref, gain_ref, wq_ref, wkv_ref,
    q_out, kv_out, lim_out,
    before, wsend, wall, seen, picked, landed, slots, lims, xall, psend, precv, squares, sqrecv,
    vis_s, vis_r, blk_s, blk_r, w_s, w_r, wf_s, wf_r, x_s, x_r, p_s, p_r, n_s, n_r,
    kx_s, kx_r, ky_s, ky_r, kc_s, kc_r,
):
    seq_count, enc_count = lax.axis_size("seq"), lax.axis_size("enc")
    s, e = lax.axis_index("seq"), lax.axis_index("enc")
    y, core, z, x = s // 2, s % 2, e // side, e % side
    ys = seq_count // 2
    rows, features = text_ref.shape
    chunks = rows // CHUNK
    window = landed.shape[1]
    vis_rows = seen.shape[1]
    columns = psend.shape[2]
    q_columns = q_out.shape[1]
    k_columns = columns - q_columns
    half = wall.shape[2] // 2
    images = count_ref.shape[0]
    twin = s + 1 - 2 * core
    mate = e + 1 - 2 * (e % 2)

    def across(k):
        return z * side + (x + k) % side

    def along(k):
        return ((z + k) % side) * side + x

    def column_of(k):
        return ((y + k) % ys) * 2 + core

    def send(source, target, ssem, rsem, to_s, to_e):
        return pltpu.make_async_remote_copy(
            src_ref=source, dst_ref=target, send_sem=ssem, recv_sem=rsem,
            device_id=(to_s, to_e), device_id_type=MESH,
        )

    barrier = pltpu.get_barrier_semaphore()

    @pl.loop(1, enc_count)
    def _(k):
        pl.semaphore_signal(barrier, inc=1, device_id=(s, (e + k) % enc_count), device_id_type=MESH)

    @pl.loop(1, seq_count)
    def _(k):
        pl.semaphore_signal(barrier, inc=1, device_id=((s + k) % seq_count, e), device_id_type=MESH)

    pl.semaphore_wait(barrier, enc_count + seq_count - 2)

    def see(k):
        to = (e + k) % enc_count
        lanes = pl.ds(pl.multiple_of(to * features, features), features)
        return send(visual_ref.at[:, lanes], seen.at[e], vis_s.at[k], vis_r.at[k], s, to)

    @pl.loop(1, enc_count)
    def _(k):
        see(k).start()

    seen[e] = visual_ref[:, pl.ds(pl.multiple_of(e * features, features), features)]

    gains = [
        spread(gain_ref[:, g * HD : (g + 1) * HD].astype(jnp.float32)) for g in range(features // HD)
    ]

    def scaled(ref, part, start):
        lanes = pl.ds(pl.multiple_of(start, HD), HD)
        block = ref[part * HD : (part + 1) * HD, lanes].astype(jnp.float32)
        return (block * gains[part]).astype(jnp.bfloat16)

    @pl.loop(0, side)
    def _(to):
        for zz in range(side):
            for part in range(features // HD):
                there = pl.ds(part * HD, HD)
                owner = zz * side + to
                for j in range(q_columns // HD):
                    wsend[to, there, pl.ds(zz * columns + j * HD, HD)] = scaled(
                        wq_ref, part, owner * q_columns + j * HD
                    )
                for j in range(k_columns // HD):
                    wsend[to, there, pl.ds(zz * columns + q_columns + j * HD, HD)] = scaled(
                        wkv_ref, part, owner * k_columns + j * HD
                    )

    mine = pl.ds(pl.multiple_of(core * half, HD), half)

    def weigh(k):
        return send(
            wsend.at[(x + k) % side, :, mine], wall.at[x, :, mine],
            w_s.at[k], w_r.at[k], s, across(k),
        )

    def pass_weights(k):
        origin = (x + side - k) % side
        return send(
            wall.at[origin, :, mine], wall.at[origin, :, mine], wf_s.at[k], wf_r.at[k], twin, e
        )

    @pl.loop(1, side)
    def _(k):
        weigh(k).start()

    wall[x] = wsend[x]

    shape = slots.shape
    position = (
        s * rows
        + lax.broadcasted_iota(jnp.int32, shape, 0) * CHUNK
        + lax.broadcasted_iota(jnp.int32, shape, 1)
    )

    def place(i, carry):
        end, offset, shift, lim, counts = carry
        start = end + gap_ref[i]
        count = count_ref[i]
        end = start + count
        inside = (position >= start) & (position < end)
        shift = jnp.where(inside, offset - start, shift)
        lim = jnp.where(inside, end - 1, lim)
        counts = tuple(
            total + jnp.minimum(jnp.maximum(b * rows - start, 0), count)
            for b, total in enumerate(counts)
        )
        return end, offset + count, shift, lim, counts

    none = jnp.full(shape, 1, jnp.int32)
    zero = jnp.int32(0)
    _, _, shift, lim, counts = lax.fori_loop(
        0, images, place, (zero, zero, none, position, (zero,) * seq_count)
    )
    for b in range(seq_count):
        before[b] = counts[b]
    lims[...] = lim.astype(jnp.float32)
    token = position + shift
    origin = (token // enc_count) % seq_count
    total = before[s]
    group = seq_count * enc_count
    skipped = (total // group) * enc_count + jnp.clip(total % group - enc_count * origin, 0, enc_count)
    slot = origin * window + (token // group) * enc_count + token % enc_count - skipped
    slots[...] = jnp.where(shift <= 0, slot, -1).astype(jnp.float32)

    @pl.loop(1, enc_count)
    def _(k):
        see(k).wait_recv()

    def one_hot(index, count):
        lane = lax.broadcasted_iota(jnp.int32, index.shape, 1).astype(jnp.float32)
        return jnp.concatenate(
            [jnp.where(index == lane + j * HD, 1.0, 0.0).astype(jnp.bfloat16) for j in range(count // HD)],
            axis=1,
        )

    def pick(b):
        total = before[b]
        skip = (total // group) * enc_count + jnp.clip(total % group - enc_count * s, 0, enc_count)
        local = skip + lax.broadcasted_iota(jnp.int32, (window, HD), 0)
        index = (local % enc_count) * vis_rows + local // enc_count
        chosen = one_hot(index.astype(jnp.float32), enc_count * vis_rows)
        table = seen[...].reshape(enc_count * vis_rows, features)
        return jnp.dot(chosen, table, preferred_element_type=jnp.float32).astype(jnp.bfloat16)

    def move(k):
        to = (s + k) % seq_count
        return send(picked.at[to], landed.at[s], blk_s.at[k], blk_r.at[k], to, e)

    @pl.loop(1, seq_count)
    def _(k):
        to = (s + k) % seq_count
        picked[to] = pick(to)
        move(k).start()

    landed[s] = pick(s)

    @pl.loop(1, side)
    def _(k):
        weigh(k).wait_recv()
        pass_weights(k).start()

    @pl.loop(1, seq_count)
    def _(k):
        move(k).wait_recv()

    def at(c):
        return pl.ds(pl.multiple_of(c * CHUNK, CHUNK), CHUNK)

    def share(k, c):
        return send(xall.at[x, at(c)], xall.at[x, at(c)], x_s.at[k, c], x_r.at[k, c], s, across(k))

    @pl.loop(0, chunks)
    def _(c):
        index = spread(slots[pl.ds(c, 1), :])
        chosen = one_hot(index, landed.shape[0] * window)
        table = landed[...].reshape(landed.shape[0] * window, features)
        frame = jnp.dot(chosen, table, preferred_element_type=jnp.float32).astype(jnp.bfloat16)
        visual = jnp.concatenate([index] * (features // HD), axis=1) >= 0
        xall[x, at(c)] = jnp.where(visual, frame, text_ref[at(c), :])
        lim_out[at(c), :] = spread(lims[pl.ds(c, 1), :])
        for k in range(1, side):
            share(k, c).start()

    @pl.loop(1, side)
    def _(k):
        pass_weights(k).wait_recv()

    def reduce(k, c):
        return send(
            psend.at[(z + k) % side, at(c)], precv.at[k, at(c)],
            p_s.at[k, c], p_r.at[k, c], s, along(k),
        )

    def norms(k, c):
        return send(squares.at[c], sqrecv.at[k, c], n_s.at[k, c], n_r.at[k, c], s, along(k))

    def keys(owner, c):
        return pl.ds(pl.multiple_of(owner * rows + c * CHUNK, CHUNK), CHUNK)

    def pair(c):
        here = kv_out.at[e % 2, keys(s, c)]
        return send(here, here, kx_s.at[c], kx_r.at[c], s, mate)

    def column(k, c):
        here = kv_out.at[:, keys(s, c)]
        return send(here, here, ky_s.at[k, c], ky_r.at[k, c], column_of(k), e)

    def chip(k, c):
        here = kv_out.at[:, keys(column_of(ys - k), c)]
        return send(here, here, kc_s.at[k, c], kc_r.at[k, c], twin, e)

    ones = jnp.ones((8, side * features), jnp.bfloat16)

    def multiply(c):
        for k in range(1, side):
            share(k, c).wait_recv()
        block = jnp.concatenate([xall[j, at(c)] for j in range(side)], axis=1)
        wide = block.astype(jnp.float32)
        squares[c] = lax.dot_general(
            ones, (wide * wide).astype(jnp.bfloat16), (((1,), (1,)), ((), ())),
            preferred_element_type=jnp.float32,
        )
        for k in range(1, side):
            norms(k, c).start()
        weights = wall[...].reshape(side * features, side * columns)
        partial = jnp.dot(block, weights, preferred_element_type=jnp.float32).astype(jnp.bfloat16)
        for zz in range(side):
            psend[zz, at(c)] = partial[:, zz * columns : (zz + 1) * columns]
        for k in range(1, side):
            reduce(k, c).start()

    def finish(c):
        total = psend[z, at(c)].astype(jnp.float32)
        square = squares[c]
        for k in range(1, side):
            reduce(k, c).wait_recv()
            norms(k, c).wait_recv()
            total = total + precv[k, at(c)].astype(jnp.float32)
            square = square + sqrecv[k, c]
        scale = spread(lax.rsqrt(square / (features * enc_count) + EPS)[0:1, :])
        factor = math.log2(math.e) / HD**0.5
        for j in range(q_columns // HD):
            lanes = slice(j * HD, (j + 1) * HD)
            q_out[at(c), lanes] = (total[:, lanes] * (scale * factor)).astype(jnp.bfloat16)
        kv_out[e % 2, keys(s, c)] = (total[:, q_columns:] * scale).astype(jnp.bfloat16)
        pair(c).start()

    def spread_out(c):
        pair(c).wait_recv()
        for k in range(1, ys):
            column(k, c).start()
        chip(0, c).start()

    def hand_over(c):
        for k in range(1, ys):
            column(k, c).wait_recv()
            chip(k, c).start()

    stages = (multiply, finish, spread_out, hand_over)
    lags = (0, 1, 2, 4)

    @pl.loop(0, chunks + lags[-1])
    def _(t):
        for stage, lag in zip(stages, lags):
            @pl.when((t >= lag) & (t < chunks + lag))
            def _():
                stage(t - lag)

    @pl.loop(0, chunks)
    def _(c):
        pair(c).wait_send()
        chip(0, c).wait()
        for k in range(1, ys):
            chip(k, c).wait()
            column(k, c).wait_send()
        for k in range(1, side):
            share(k, c).wait_send()
            reduce(k, c).wait_send()
            norms(k, c).wait_send()

    @pl.loop(1, side)
    def _(k):
        weigh(k).wait_send()
        pass_weights(k).wait_send()

    @pl.loop(1, enc_count)
    def _(k):
        see(k).wait_send()

    @pl.loop(1, seq_count)
    def _(k):
        move(k).wait_send()


def project(text, visual, gain, w_query, w_keyval, image_count, text_gap):
    rows, features = text.shape
    vis_rows = visual.shape[0]
    seq_count, enc_count = lax.axis_size("seq"), lax.axis_size("enc")
    side, ys = math.isqrt(enc_count), seq_count // 2
    q_columns = w_query.shape[1] // enc_count
    columns = q_columns + w_keyval.shape[1] // enc_count
    chunks = rows // CHUNK
    window = rows // seq_count
    bf16, f32 = jnp.bfloat16, jnp.float32

    def dma(*shape):
        return [pltpu.SemaphoreType.DMA(shape)] * 2

    return pl.pallas_call(
        functools.partial(project_kernel, side),
        out_shape=(
            jax.ShapeDtypeStruct((rows, q_columns), bf16),
            jax.ShapeDtypeStruct((2, rows * seq_count, HD), bf16),
            jax.ShapeDtypeStruct((rows, HD), f32),
        ),
        in_specs=[pl.BlockSpec(memory_space=pltpu.SMEM)] * 2 + [pl.BlockSpec(memory_space=VMEM)] * 5,
        out_specs=tuple([pl.BlockSpec(memory_space=VMEM)] * 3),
        scratch_shapes=[
            pltpu.SMEM((seq_count,), jnp.int32),
            VMEM((side, features, side * columns), bf16),
            VMEM((side, features, side * columns), bf16),
            VMEM((enc_count, vis_rows, features), bf16),
            VMEM((seq_count, window, features), bf16),
            VMEM((seq_count, window, features), bf16),
            VMEM((16, HD), f32),
            VMEM((16, HD), f32),
            VMEM((side, rows, features), bf16),
            VMEM((side, rows, columns), bf16),
            VMEM((side, rows, columns), bf16),
            VMEM((chunks, 8, CHUNK), f32),
            VMEM((side, chunks, 8, CHUNK), f32),
            *dma(enc_count),
            *dma(seq_count),
            *dma(side),
            *dma(side),
            *dma(side, chunks),
            *dma(side, chunks),
            *dma(side, chunks),
            *dma(chunks),
            *dma(ys, chunks),
            *dma(ys, chunks),
        ],
        compiler_params=pltpu.CompilerParams(
            collective_id=0, has_side_effects=True, vmem_limit_bytes=60 << 20
        ),
    )(image_count, text_gap, text, visual, gain, w_query, w_keyval)


def attention_kernel(bq, bk, sbq, sbk, off_ref, q_ref, kv_ref, lim_ref, o_ref, acc, den, top):
    heads = q_ref.shape[1] // HD
    rows_all, keys_all = q_ref.shape[0], kv_ref.shape[1]
    q0 = off_ref[0]

    def query_norm(step, best):
        block = q_ref[pl.ds(pl.multiple_of(step * 128, 128), 128), :].astype(jnp.float32)
        square = block * block
        for head in range(heads):
            norm = jnp.sum(square[:, head * HD : (head + 1) * HD], axis=1, keepdims=True)
            best = jnp.maximum(best, norm)
        return best

    def key_norm(step, best):
        block = kv_ref[0, pl.ds(pl.multiple_of(step * 128, 128), 128), :].astype(jnp.float32)
        return jnp.maximum(best, jnp.sum(block * block, axis=1, keepdims=True))

    zero = jnp.zeros((128, 1), jnp.float32)
    largest_query = jnp.max(lax.fori_loop(0, rows_all // 128, query_norm, zero))
    largest_key = jnp.max(lax.fori_loop(0, keys_all // 128, key_norm, zero))
    safe = largest_query * largest_key < SAFE * SAFE

    def scores(row, head, size, key, count, masked):
        q = q_ref[pl.ds(row, size), head * HD : (head + 1) * HD]
        s = lax.dot_general(
            q,
            kv_ref[0, pl.ds(key, count), :],
            (((1,), (1,)), ((), ())),
            preferred_element_type=jnp.float32,
        )
        if masked:
            at = (key + lax.broadcasted_iota(jnp.int32, (size, count), 1)).astype(jnp.float32)
            lim = jnp.concatenate([lim_ref[pl.ds(row, size), :]] * (count // HD), axis=1)
            s = jnp.where(at <= lim, s, NEG)
        return s

    def lane_sums(p):
        total = p[:, :HD]
        for part in range(1, p.shape[1] // HD):
            total = total + p[:, part * HD : (part + 1) * HD]
        return total

    def tiles(size, count, begin, step, end):
        @pl.loop(0, rows_all // size)
        def _(tile):
            row = pl.multiple_of(tile * size, size)
            begin()
            first = q0 + row
            whole = first // count
            last = jnp.minimum(pl.cdiv(first + size + 255, count), keys_all // count)

            @pl.loop(0, whole)
            def _(j):
                step(row, pl.multiple_of(j * count, count), False)

            @pl.loop(whole, last)
            def _(j):
                step(row, pl.multiple_of(j * count, count), True)

            end(row)

    @pl.when(safe)
    def _():
        def begin():
            acc[...] = jnp.zeros_like(acc)
            den[...] = jnp.zeros_like(den)

        def step(row, key, masked):
            values = kv_ref[1, pl.ds(key, bk), :]
            for head in range(heads):
                p = jnp.exp2(scores(row, head, bq, key, bk, masked))
                acc[head] += jnp.dot(
                    p.astype(jnp.bfloat16), values, preferred_element_type=jnp.float32
                )
                den[head] += lane_sums(p)

        def end(row):
            for head in range(heads):
                result = acc[head] / jnp.sum(den[head], axis=1, keepdims=True)
                o_ref[pl.ds(row, bq), head * HD : (head + 1) * HD] = result.astype(jnp.bfloat16)

        tiles(bq, bk, begin, step, end)

    @pl.when(jnp.logical_not(safe))
    def _():
        part = pl.ds(0, sbq)

        def begin():
            acc[...] = jnp.zeros_like(acc)
            den[...] = jnp.zeros_like(den)
            top[...] = jnp.full_like(top, NEG)

        def step(row, key, masked):
            values = kv_ref[1, pl.ds(key, sbk), :]
            for head in range(heads):
                s = scores(row, head, sbq, key, sbk, masked)
                old = top[head]
                new = jnp.maximum(old, jnp.max(s, axis=1, keepdims=True))
                top[head] = new
                p = jnp.exp2(s - new)
                shrink = jnp.exp2(old - new)
                acc[head, part] = acc[head, part] * shrink + jnp.dot(
                    p.astype(jnp.bfloat16), values, preferred_element_type=jnp.float32
                )
                den[head, part] = den[head, part] * shrink + lane_sums(p)

        def end(row):
            for head in range(heads):
                result = acc[head, part] / jnp.sum(den[head, part], axis=1, keepdims=True)
                o_ref[pl.ds(row, sbq), head * HD : (head + 1) * HD] = result.astype(jnp.bfloat16)

        tiles(sbq, sbk, begin, step, end)


def attention(q0, query, keyval, lim):
    rows, width = query.shape
    heads = width // HD
    bq, bk, sbq, sbk = rows // 2, 1024, 128, 512
    flops = 4 * rows * keyval.shape[1] * width
    return pl.pallas_call(
        functools.partial(attention_kernel, bq, bk, sbq, sbk),
        out_shape=jax.ShapeDtypeStruct(query.shape, jnp.bfloat16),
        in_specs=[pl.BlockSpec(memory_space=pltpu.SMEM)] + [pl.BlockSpec(memory_space=VMEM)] * 3,
        out_specs=pl.BlockSpec(memory_space=VMEM),
        scratch_shapes=[
            VMEM((heads, bq, HD), jnp.float32),
            VMEM((heads, bq, HD), jnp.float32),
            VMEM((heads, sbq, 1), jnp.float32),
        ],
        compiler_params=pltpu.CompilerParams(vmem_limit_bytes=56 << 20),
        cost_estimate=pl.CostEstimate(
            flops=flops, bytes_accessed=keyval.size * 2, transcendentals=rows * keyval.shape[1]
        ),
    )(q0, query, keyval, lim)


def per_device(text, visual, gain, w_query, w_keyval, image_count, text_gap):
    rows = text.shape[0]
    visual = jnp.pad(visual, ((0, -visual.shape[0] % 16), (0, 0)))
    query, keyval, lim = project(
        text, visual, gain[None, :], w_query, w_keyval, image_count, text_gap
    )
    q0 = (lax.axis_index("seq") * rows).astype(jnp.int32).reshape(1)
    return attention(q0, query, keyval, lim)


def solution(mesh):
    in_specs = (
        P("seq", "enc"),
        P(("seq", "enc"), None),
        P("enc"),
        P("enc", None),
        P("enc", None),
        P(),
        P(),
    )
    out_specs = P("seq", "enc")
    return jax.shard_map(
        per_device, mesh=mesh, in_specs=in_specs, out_specs=out_specs, check_vma=False
    )
```

time: 417 us -> 287 us (0.69)
  Pallas kernels: 178 us -> 283 us
  blocking collectives: 89 us -> 0 us
  waiting for transfers between devices: 68.6 us -> 0 us
  between operations: 28.3 us -> 0.01 us
  local copies, waits for them, and re-layouts: 23.3 us -> 2.97 us
  starting transfers between devices: 10.8 us -> 0 us
  other arithmetic: 9.16 us -> 0 us
  matrix products: 8.79 us -> 0 us
    pallas_call x1, Pallas kernels: 6.33 us -> 112 us  [project(): pl.pallas_call(functools.partial(project_kernel, side), out_shape=(jax.Sh...]
    all_to_all x1 -> x0, blocking collectives: 59.2 us -> none  [per_device(): lax.all_to_all(w, 'enc', split_axis=0, concat_axis=0, axis_index_groups=n...]
    all_gather x2 -> x0, waiting for transfers between devices: 32.6 us -> none  [the longest x1 32.6 us: per_device(): keyval = lax.all_gather(keyval, 'seq', axis=0, tiled=True)]
    psum x1 -> x0, blocking collectives: 29.8 us -> none  [per_device(): square = lax.psum(jnp.sum(widened * widened, axis=1), 'enc')]
    unnamed x25 -> x0, local copies, waits for them, and re-layouts: 14.8 us -> none
    all_to_all x1 -> x0, waiting for transfers between devices: 14.7 us -> none  [per_device(): lax.all_to_all(pieces, ('seq', 'enc'), split_axis=0, concat_axis=0, tiled...]
    unnamed x4 -> x0, waiting for transfers between devices: 12.6 us -> none
    all_to_all x1 -> x0, starting transfers between devices: 10.6 us -> none  [per_device(): lax.all_to_all(pieces, ('seq', 'enc'), split_axis=0, concat_axis=0, tiled...]
  transfers between devices with their start and end apart: 5 -> 0, of which waited for: 4 -> 0; matrix products, arithmetic and copies ran while one was open for 3% -> 0% of each run, Pallas kernels for 0% -> 0%
where the time goes in v2:
time: 287 us; the launch traced here: 286 us
  Pallas kernels  283 us (99%)
  local copies, waits for them, and re-layouts  2.97 us (1%)
    pallas_call x1, Pallas kernels, attention(): pl.pallas_call(functools.partial(attention_kernel, bq, bk, sbq, sbk), out...  171 us
    pallas_call x1, Pallas kernels, project(): pl.pallas_call(functools.partial(project_kernel, side), out_shape=(jax.Sh...  112 us

profile of v2, /device:TPU:25, one launch (start us, length us, event | category | flops | bytes accessed | tf_op | source)
XLA Modules:
  0.0 285.9 jit_solution(3589692226667459296)
XLA Ops:
  0.0 1.2 broadcast_in_dim.3.gain_ref
  1.2 1.7 pad.4.visual_ref
  3.0 111.5 %shard_map.73 = (bf16[1280,256]{1,0:T(8,128)(2,1)}, bf16[2,10240,128]{2,1,0:T(8,128)(2,1)}, f32[1280,128]{1,0:T(8,128)}) custom-call(s32[32]{0:T(128)} %count_ref.1, s32[33]{0:T(128)} %gap_ref.1, bf16[1280,256]{1,0:T(8,128)(2,1)} %text_ref.1, bf16[48,4096]{1,0:T(8,128)(2,1)} %pad.4.visual_ref, bf16[1,256]{1,0:T(2,128)(2,1)} %broadcast_in_dim.3.gain_ref, ...), custom_call_target="tpu_custom_call" | custom-call | tf_op jit(solution)/shard_map/pallas_call | solution.py:350
  114.5 171.4 %shard_map.74 = bf16[1280,256]{1,0:T(8,128)(2,1)} custom-call(s32[1]{0:T(128)} %bitcast.off_ref, bf16[1280,256]{1,0:T(8,128)(2,1)} %get-tuple-element.8.q_ref, bf16[2,10240,128]{2,1,0:T(8,128)(2,1)} %get-tuple-element.9.kv_ref, f32[1280,128]{1,0:T(8,128)} %get-tuple-element.10.lim_ref), custom_call_target="tpu_custom_call" | custom-call | flops 13421772800 | bytes 5242880 | tf_op jit(solution)/shard_map/pallas_call | solution.py:509

commit v3 on v2

--- a/solution.py
+++ b/solution.py
@@ -24,9 +24,10 @@
 def project_kernel(
     side, count_ref, gap_ref, text_ref, visual_ref, gain_ref, wq_ref, wkv_ref,
     q_out, kv_out, lim_out,
-    before, wsend, wall, seen, picked, landed, slots, lims, xall, psend, precv, squares, sqrecv,
-    vis_s, vis_r, blk_s, blk_r, w_s, w_r, wf_s, wf_r, x_s, x_r, p_s, p_r, n_s, n_r,
-    kx_s, kx_r, ky_s, ky_r, kc_s, kc_r,
+    before, wsend, wall, seen, picked, landed, slots, lims, xall, psend, pmid, precv, squares,
+    sqrecv, qown,
+    vis_s, vis_r, blk_s, blk_r, w_s, w_r, wf_s, wf_r, x_s, x_r, xf_s, xf_r, p_s, p_r, pf_s, pf_r,
+    n_s, n_r, kx_s, kx_r, ky_s, ky_r, kc_s, kc_r, q_s, q_r,
 ):
     seq_count, enc_count = lax.axis_size("seq"), lax.axis_size("enc")
     s, e = lax.axis_index("seq"), lax.axis_index("enc")
@@ -43,6 +44,8 @@
     images = count_ref.shape[0]
     twin = s + 1 - 2 * core
     mate = e + 1 - 2 * (e % 2)
+    other = seq_count - 1 - s
+    sides = (1, side - 1)
 
     def across(k):
         return z * side + (x + k) % side
@@ -59,6 +62,7 @@
             device_id=(to_s, to_e), device_id_type=MESH,
         )
 
+    seen[...] = jnp.zeros_like(seen)
     barrier = pltpu.get_barrier_semaphore()
 
     @pl.loop(1, enc_count)
@@ -74,16 +78,22 @@
     def see(k):
         to = (e + k) % enc_count
         lanes = pl.ds(pl.multiple_of(to * features, features), features)
-        return send(visual_ref.at[:, lanes], seen.at[e], vis_s.at[k], vis_r.at[k], s, to)
+        there = seen.at[e, pl.ds(0, visual_ref.shape[0])]
+        return send(visual_ref.at[:, lanes], there, vis_s.at[k], vis_r.at[k], s, to)
 
     @pl.loop(1, enc_count)
     def _(k):
         see(k).start()
 
-    seen[e] = visual_ref[:, pl.ds(pl.multiple_of(e * features, features), features)]
+    kept = pltpu.make_async_copy(
+        visual_ref.at[:, pl.ds(pl.multiple_of(e * features, features), features)],
+        seen.at[e, pl.ds(0, visual_ref.shape[0])],
+        vis_s.at[0],
+    )
+    kept.start()
 
     gains = [
-        spread(gain_ref[:, g * HD : (g + 1) * HD].astype(jnp.float32)) for g in range(features // HD)
+        spread(gain_ref[g * HD : (g + 1) * HD].astype(jnp.float32).reshape(1, HD)) for g in range(features // HD)
     ]
 
     def scaled(ref, part, start):
@@ -133,6 +143,10 @@
         + lax.broadcasted_iota(jnp.int32, shape, 1)
     )
 
+    seat = jnp.where(
+        lax.broadcasted_iota(jnp.int32, shape, 0) >= chunks // 2, position, position + (other - s) * rows
+    )
+
     def place(i, carry):
         end, offset, shift, lim, counts = carry
         start = end + gap_ref[i]
@@ -140,7 +154,7 @@
         end = start + count
         inside = (position >= start) & (position < end)
         shift = jnp.where(inside, offset - start, shift)
-        lim = jnp.where(inside, end - 1, lim)
+        lim = jnp.where((seat >= start) & (seat < end), end - 1, lim)
         counts = tuple(
             total + jnp.minimum(jnp.maximum(b * rows - start, 0), count)
             for b, total in enumerate(counts)
@@ -150,7 +164,7 @@
     none = jnp.full(shape, 1, jnp.int32)
     zero = jnp.int32(0)
     _, _, shift, lim, counts = lax.fori_loop(
-        0, images, place, (zero, zero, none, position, (zero,) * seq_count)
+        0, images, place, (zero, zero, none, seat, (zero,) * seq_count)
     )
     for b in range(seq_count):
         before[b] = counts[b]
@@ -167,6 +181,8 @@
     def _(k):
         see(k).wait_recv()
 
+    kept.wait()
+
     def one_hot(index, count):
         lane = lax.broadcasted_iota(jnp.int32, index.shape, 1).astype(jnp.float32)
         return jnp.concatenate(
@@ -207,11 +223,52 @@
     def at(c):
         return pl.ds(pl.multiple_of(c * CHUNK, CHUNK), CHUNK)
 
+    def half_of(k, c):
+        return pl.ds(pl.multiple_of(c * CHUNK + (k // 2) * (CHUNK // 2), CHUNK // 2), CHUNK // 2)
+
     def share(k, c):
         return send(xall.at[x, at(c)], xall.at[x, at(c)], x_s.at[k, c], x_r.at[k, c], s, across(k))
 
-    @pl.loop(0, chunks)
-    def _(c):
+    def relay(k, c):
+        here = xall.at[(x + side - k) % side, half_of(k, c)]
+        return send(here, here, xf_s.at[k, c], xf_r.at[k, c], s, across(k))
+
+    def reach(k, c):
+        return send(
+            psend.at[(z + side // 2) % side, half_of(k, c)], pmid.at[half_of(k, c)],
+            pf_s.at[k, c], pf_r.at[k, c], s, along(k),
+        )
+
+    def reduce(k, c):
+        return send(
+            psend.at[(z + k) % side, at(c)], precv.at[k // 2, at(c)],
+            p_s.at[k, c], p_r.at[k, c], s, along(k),
+        )
+
+    def trade(c):
+        return send(qown.at[at(c)], q_out.at[at(c)], q_s.at[c], q_r.at[c], other, e)
+
+    def norms(k, c):
+        return send(squares.at[c], sqrecv.at[k, c], n_s.at[k, c], n_r.at[k, c], s, along(k))
+
+    def keys(owner, c):
+        return pl.ds(pl.multiple_of(owner * rows + c * CHUNK, CHUNK), CHUNK)
+
+    def pair(c):
+        here = kv_out.at[e % 2, keys(s, c)]
+        return send(here, here, kx_s.at[c], kx_r.at[c], s, mate)
+
+    def column(k, c):
+        here = kv_out.at[:, keys(s, c)]
+        return send(here, here, ky_s.at[k, c], ky_r.at[k, c], column_of(k), e)
+
+    def chip(k, c):
+        here = kv_out.at[:, keys(column_of(ys - k), c)]
+        return send(here, here, kc_s.at[k, c], kc_r.at[k, c], twin, e)
+
+    ones = jnp.ones((8, side * features), jnp.bfloat16)
+
+    def push(c):
         index = spread(slots[pl.ds(c, 1), :])
         chosen = one_hot(index, landed.shape[0] * window)
         table = landed[...].reshape(landed.shape[0] * window, features)
@@ -219,42 +276,22 @@
         visual = jnp.concatenate([index] * (features // HD), axis=1) >= 0
         xall[x, at(c)] = jnp.where(visual, frame, text_ref[at(c), :])
         lim_out[at(c), :] = spread(lims[pl.ds(c, 1), :])
-        for k in range(1, side):
+        for k in sides:
             share(k, c).start()
 
-    @pl.loop(1, side)
-    def _(k):
-        pass_weights(k).wait_recv()
-
-    def reduce(k, c):
-        return send(
-            psend.at[(z + k) % side, at(c)], precv.at[k, at(c)],
-            p_s.at[k, c], p_r.at[k, c], s, along(k),
-        )
-
-    def norms(k, c):
-        return send(squares.at[c], sqrecv.at[k, c], n_s.at[k, c], n_r.at[k, c], s, along(k))
-
-    def keys(owner, c):
-        return pl.ds(pl.multiple_of(owner * rows + c * CHUNK, CHUNK), CHUNK)
-
-    def pair(c):
-        here = kv_out.at[e % 2, keys(s, c)]
-        return send(here, here, kx_s.at[c], kx_r.at[c], s, mate)
-
-    def column(k, c):
-        here = kv_out.at[:, keys(s, c)]
-        return send(here, here, ky_s.at[k, c], ky_r.at[k, c], column_of(k), e)
-
-    def chip(k, c):
-        here = kv_out.at[:, keys(column_of(ys - k), c)]
-        return send(here, here, kc_s.at[k, c], kc_r.at[k, c], twin, e)
-
-    ones = jnp.ones((8, side * features), jnp.bfloat16)
+    def hop(c):
+        for k in sides:
+            share(k, c).wait_recv()
+            relay(k, c).start()
 
     def multiply(c):
-        for k in range(1, side):
-            share(k, c).wait_recv()
+        @pl.when(c == 0)
+        def _():
+            for k in range(1, side):
+                pass_weights(k).wait_recv()
+
+        for k in sides:
+            relay(k, c).wait_recv()
         block = jnp.concatenate([xall[j, at(c)] for j in range(side)], axis=1)
         wide = block.astype(jnp.float32)
         squares[c] = lax.dot_general(
@@ -267,22 +304,41 @@
         partial = jnp.dot(block, weights, preferred_element_type=jnp.float32).astype(jnp.bfloat16)
         for zz in range(side):
             psend[zz, at(c)] = partial[:, zz * columns : (zz + 1) * columns]
-        for k in range(1, side):
+        for k in sides:
+            reach(k, c).start()
+
+    def merge(c):
+        for k in sides:
+            reach(k, c).wait_recv()
+            rows_here = half_of(k, c)
+            target = (z + k) % side
+            joined = psend[target, rows_here].astype(jnp.float32) + pmid[rows_here].astype(jnp.float32)
+            psend[target, rows_here] = joined.astype(jnp.bfloat16)
             reduce(k, c).start()
 
     def finish(c):
         total = psend[z, at(c)].astype(jnp.float32)
         square = squares[c]
+        for k in sides:
+            reduce(k, c).wait_recv()
+            total = total + precv[k // 2, at(c)].astype(jnp.float32)
         for k in range(1, side):
-            reduce(k, c).wait_recv()
             norms(k, c).wait_recv()
-            total = total + precv[k, at(c)].astype(jnp.float32)
             square = square + sqrecv[k, c]
         scale = spread(lax.rsqrt(square / (features * enc_count) + EPS)[0:1, :])
         factor = math.log2(math.e) / HD**0.5
         for j in range(q_columns // HD):
             lanes = slice(j * HD, (j + 1) * HD)
-            q_out[at(c), lanes] = (total[:, lanes] * (scale * factor)).astype(jnp.bfloat16)
+            qown[at(c), lanes] = (total[:, lanes] * (scale * factor)).astype(jnp.bfloat16)
+
+        @pl.when(c >= chunks // 2)
+        def _():
+            q_out[at(c), :] = qown[at(c), :]
+
+        @pl.when(c < chunks // 2)
+        def _():
+            trade(c).start()
+
         kv_out[e % 2, keys(s, c)] = (total[:, q_columns:] * scale).astype(jnp.bfloat16)
         pair(c).start()
 
@@ -297,8 +353,8 @@
             column(k, c).wait_recv()
             chip(k, c).start()
 
-    stages = (multiply, finish, spread_out, hand_over)
-    lags = (0, 1, 2, 4)
+    stages = (push, hop, multiply, merge, finish, spread_out, hand_over)
+    lags = (0, 2, 3, 4, 5, 6, 8)
 
     @pl.loop(0, chunks + lags[-1])
     def _(t):
@@ -314,10 +370,17 @@
         for k in range(1, ys):
             chip(k, c).wait()
             column(k, c).wait_send()
+        for k in sides:
+            share(k, c).wait_send()
+            relay(k, c).wait_send()
+            reach(k, c).wait_send()
+            reduce(k, c).wait_send()
         for k in range(1, side):
-            share(k, c).wait_send()
-            reduce(k, c).wait_send()
             norms(k, c).wait_send()
+
+    @pl.loop(0, chunks // 2)
+    def _(c):
+        trade(c).wait()
 
     @pl.loop(1, side)
     def _(k):
@@ -335,7 +398,7 @@
 
 def project(text, visual, gain, w_query, w_keyval, image_count, text_gap):
     rows, features = text.shape
-    vis_rows = visual.shape[0]
+    vis_rows = pl.cdiv(visual.shape[0], 16) * 16
     seq_count, enc_count = lax.axis_size("seq"), lax.axis_size("enc")
     side, ys = math.isqrt(enc_count), seq_count // 2
     q_columns = w_query.shape[1] // enc_count
@@ -354,7 +417,9 @@
             jax.ShapeDtypeStruct((2, rows * seq_count, HD), bf16),
             jax.ShapeDtypeStruct((rows, HD), f32),
         ),
-        in_specs=[pl.BlockSpec(memory_space=pltpu.SMEM)] * 2 + [pl.BlockSpec(memory_space=VMEM)] * 5,
+        in_specs=[pl.BlockSpec(memory_space=pltpu.SMEM)] * 2
+        + [pl.BlockSpec(memory_space=VMEM), pl.BlockSpec(memory_space=pl.ANY)]
+        + [pl.BlockSpec(memory_space=VMEM)] * 3,
         out_specs=tuple([pl.BlockSpec(memory_space=VMEM)] * 3),
         scratch_shapes=[
             pltpu.SMEM((seq_count,), jnp.int32),
@@ -367,9 +432,11 @@
             VMEM((16, HD), f32),
             VMEM((side, rows, features), bf16),
             VMEM((side, rows, columns), bf16),
-            VMEM((side, rows, columns), bf16),
+            VMEM((rows, columns), bf16),
+            VMEM((2, rows, columns), bf16),
             VMEM((chunks, 8, CHUNK), f32),
             VMEM((side, chunks, 8, CHUNK), f32),
+            VMEM((rows, q_columns), bf16),
             *dma(enc_count),
             *dma(seq_count),
             *dma(side),
@@ -377,9 +444,12 @@
             *dma(side, chunks),
             *dma(side, chunks),
             *dma(side, chunks),
+            *dma(side, chunks),
+            *dma(side, chunks),
             *dma(chunks),
             *dma(ys, chunks),
             *dma(ys, chunks),
+            *dma(chunks),
         ],
         compiler_params=pltpu.CompilerParams(
             collective_id=0, has_side_effects=True, vmem_limit_bytes=60 << 20
@@ -400,14 +470,17 @@
             best = jnp.maximum(best, norm)
         return best
 
+    ones = jnp.ones((HD, HD), jnp.bfloat16)
+
     def key_norm(step, best):
-        block = kv_ref[0, pl.ds(pl.multiple_of(step * 128, 128), 128), :].astype(jnp.float32)
-        return jnp.maximum(best, jnp.sum(block * block, axis=1, keepdims=True))
+        block = kv_ref[0, pl.ds(pl.multiple_of(step * bk, bk), bk), :]
+        norm = jnp.dot(block * block, ones, preferred_element_type=jnp.float32)
+        return jnp.maximum(best, jnp.max(norm.reshape(bk // 8, 8, HD), axis=0))
 
     zero = jnp.zeros((128, 1), jnp.float32)
     largest_query = jnp.max(lax.fori_loop(0, rows_all // 128, query_norm, zero))
-    largest_key = jnp.max(lax.fori_loop(0, keys_all // 128, key_norm, zero))
-    safe = largest_query * largest_key < SAFE * SAFE
+    largest_key = jnp.max(lax.fori_loop(0, keys_all // bk, key_norm, jnp.zeros((8, HD), jnp.float32)))
+    safe = largest_query * largest_key * 1.02 < SAFE * SAFE
 
     def scores(row, head, size, key, count, masked):
         q = q_ref[pl.ds(row, size), head * HD : (head + 1) * HD]
@@ -501,15 +574,21 @@
         tiles(sbq, sbk, begin, step, end)
 
 
-def attention(q0, query, keyval, lim):
-    rows, width = query.shape
+def attention(q0, query, keyval, lim, part):
+    rows, width = query.shape[0] // 2, query.shape[1]
     heads = width // HD
-    bq, bk, sbq, sbk = rows // 2, 1024, 128, 512
+    bq, bk, sbq, sbk = rows, 1024, 128, 512
     flops = 4 * rows * keyval.shape[1] * width
     return pl.pallas_call(
         functools.partial(attention_kernel, bq, bk, sbq, sbk),
-        out_shape=jax.ShapeDtypeStruct(query.shape, jnp.bfloat16),
-        in_specs=[pl.BlockSpec(memory_space=pltpu.SMEM)] + [pl.BlockSpec(memory_space=VMEM)] * 3,
+        out_shape=jax.ShapeDtypeStruct((rows, width), jnp.bfloat16),
+        grid=(1,),
+        in_specs=[
+            pl.BlockSpec(memory_space=pltpu.SMEM),
+            pl.BlockSpec((rows, width), lambda i: (part, 0)),
+            pl.BlockSpec(memory_space=VMEM),
+            pl.BlockSpec((rows, HD), lambda i: (part, 0)),
+        ],
         out_specs=pl.BlockSpec(memory_space=VMEM),
         scratch_shapes=[
             VMEM((heads, bq, HD), jnp.float32),
@@ -525,12 +604,17 @@
 
 def per_device(text, visual, gain, w_query, w_keyval, image_count, text_gap):
     rows = text.shape[0]
-    visual = jnp.pad(visual, ((0, -visual.shape[0] % 16), (0, 0)))
     query, keyval, lim = project(
-        text, visual, gain[None, :], w_query, w_keyval, image_count, text_gap
+        text, visual, gain, w_query, w_keyval, image_count, text_gap
     )
-    q0 = (lax.axis_index("seq") * rows).astype(jnp.int32).reshape(1)
-    return attention(q0, query, keyval, lim)
+    half = rows // 2
+    seq_count = lax.axis_size("seq")
+    mine = (lax.axis_index("seq") * rows).astype(jnp.int32)
+    theirs = (seq_count - 1) * rows - mine
+    lent = attention(theirs.reshape(1), query, keyval, lim, 0)
+    back = lax.ppermute(lent, "seq", [(i, seq_count - 1 - i) for i in range(seq_count)])
+    own = attention((mine + half).reshape(1), query, keyval, lim, 1)
+    return jnp.concatenate((back, own), axis=0)
 
 
 def solution(mesh):

time: 287 us -> 275 us (0.958)
  Pallas kernels: 283 us -> 200 us
  starting transfers between devices: 0 us -> 72.5 us
  local copies, waits for them, and re-layouts: 2.97 us -> 0 us
    ppermute x0 -> x1, starting transfers between devices: none -> 72.5 us  [per_device(): lax.ppermute(lent, 'seq', [(i, seq_count - 1 - i) for i in range(seq_coun...]
    pallas_call x1 -> x2, Pallas kernels: 171 us -> 101 us  [attention(): pl.pallas_call(functools.partial(attention_kernel, bq, bk, sbq, sbk), out...]
    pallas_call x1, Pallas kernels: 112 us -> 98.5 us  [project(): pl.pallas_call(functools.partial(project_kernel, side), out_shape=(jax.Sh...]
  transfers between devices with their start and end apart: 0 -> 1, of which waited for: 0 -> 0; matrix products, arithmetic and copies ran while one was open for 0% -> 0% of each run, Pallas kernels for 0% -> 32%
where the time goes in v3:
time: 275 us; the launch traced here: 274 us
  Pallas kernels  200 us (73%)
  starting transfers between devices  72.5 us (26%)
    pallas_call x2, Pallas kernels, attention(): pl.pallas_call(functools.partial(attention_kernel, bq, bk, sbq, sbk), out...  101 us
    pallas_call x1, Pallas kernels, project(): pl.pallas_call(functools.partial(project_kernel, side), out_shape=(jax.Sh...  98.5 us
    ppermute x1, starting transfers between devices, per_device(): lax.ppermute(lent, 'seq', [(i, seq_count - 1 - i) for i in range(seq_coun...  72.5 us
  transfers between devices with their start and end apart: 1, of which 0 were waited for; matrix products, arithmetic and copies ran while one was open for 0% of the time, Pallas kernels for 32%

profile of v3, /device:TPU:25, one launch (start us, length us, event | category | flops | bytes accessed | tf_op | source)
XLA Modules:
  0.0 274.5 jit_solution(14828599791030982798)
XLA Ops:
  0.0 98.5 %shard_map.73 = (bf16[1280,256]{1,0:T(8,128)(2,1)}, bf16[2,10240,128]{2,1,0:T(8,128)(2,1)}, f32[1280,128]{1,0:T(8,128)}) custom-call(s32[32]{0:T(128)} %count_ref.1, s32[33]{0:T(128)} %gap_ref.1, bf16[1280,256]{1,0:T(8,128)(2,1)} %text_ref.1, bf16[40,4096]{1,0:T(8,128)(2,1)} %visual_ref.1, bf16[256]{0:T(256)(128)(2,1)} %gain_ref.1, ...), custom_call_target="tpu_custom_call" | custom-call | tf_op jit(solution)/shard_map/pallas_call | solution.py:413
  98.6 13.9 %shard_map.74 = bf16[640,256]{1,0:T(8,128)(2,1)} custom-call(s32[1]{0:T(128)} %bitcast.off_ref, bf16[1280,256]{1,0:T(8,128)(2,1)} %get-tuple-element.8.q_ref, bf16[2,10240,128]{2,1,0:T(8,128)(2,1)} %get-tuple-element.9.kv_ref, f32[1280,128]{1,0:T(8,128)} %get-tuple-element.10.lim_ref), custom_call_target="tpu_custom_call" | custom-call | flops 6710886400 | bytes 5242880 | tf_op jit(solution)/shard_map/pallas_call | solution.py:582
  112.5 72.5 %collective-permute-start = (bf16[640,256]{1,0:T(8,128)(2,1)}, bf16[640,256]{1,0:T(8,128)(2,1)S(1)}, u32[]{:S(2)}, u32[]{:S(2)}) collective-permute-start(bf16[640,256]{1,0:T(8,128)(2,1)} %shard_map.74), channel_id=1, source_target_pairs={{0,112},{16,96},{32,80},{48,64},{64,48},{80,32},{96,16},{112,0},{1... | collective-permute-start | bytes 983048 | tf_op jit(solution)/shard_map/ppermute | solution.py:615
  185.0 87.6 %shard_map.75 = bf16[640,256]{1,0:T(8,128)(2,1)} custom-call(s32[1]{0:T(128)} %bitcast.1.off_ref, bf16[1280,256]{1,0:T(8,128)(2,1)} %get-tuple-element.8.q_ref, bf16[2,10240,128]{2,1,0:T(8,128)(2,1)} %get-tuple-element.9.kv_ref, f32[1280,128]{1,0:T(8,128)} %get-tuple-element.10.lim_ref), custom_call_target="tpu_custom_call" | custom-call | flops 6710886400 | bytes 5242880 | tf_op jit(solution)/shard_map/pallas_call | solution.py:582
  272.6 0.0 collective-permute-done
  272.6 1.9 pad_maximum_fusion
Async XLA Ops:
  112.5 160.1 %collective-permute-start = (bf16[640,256]{1,0:T(8,128)(2,1)}, bf16[640,256]{1,0:T(8,128)(2,1)S(1)}, u32[]{:S(2)}, u32[]{:S(2)}) collective-permute-start(bf16[640,256]{1,0:T(8,128)(2,1)} %shard_map.74), channel_id=1, source_target_pairs={{0,112},{16,96},{32,80},{48,64},{64,48},{80,32},{96,16},{112,0},{1... | collective-permute-start | bytes 983048 | tf_op jit(solution)/shard_map/ppermute | solution.py:615

commit v4 on v3

--- a/solution.py
+++ b/solution.py
@@ -23,11 +23,11 @@
 
 def project_kernel(
     side, count_ref, gap_ref, text_ref, visual_ref, gain_ref, wq_ref, wkv_ref,
-    q_out, kv_out, lim_out,
+    q_out, kv_out, lim_out, safe_out,
     before, wsend, wall, seen, picked, landed, slots, lims, xall, psend, pmid, precv, squares,
-    sqrecv, qown,
+    sqrecv, qown, peak, peaks,
     vis_s, vis_r, blk_s, blk_r, w_s, w_r, wf_s, wf_r, x_s, x_r, xf_s, xf_r, p_s, p_r, pf_s, pf_r,
-    n_s, n_r, kx_s, kx_r, ky_s, ky_r, kc_s, kc_r, q_s, q_r,
+    n_s, n_r, kx_s, kx_r, ky_s, ky_r, kc_s, kc_r, q_s, q_r, m_s, m_r,
 ):
     seq_count, enc_count = lax.axis_size("seq"), lax.axis_size("enc")
     s, e = lax.axis_index("seq"), lax.axis_index("enc")
@@ -327,9 +327,13 @@
             square = square + sqrecv[k, c]
         scale = spread(lax.rsqrt(square / (features * enc_count) + EPS)[0:1, :])
         factor = math.log2(math.e) / HD**0.5
+        query_norm = jnp.zeros((CHUNK, 1), jnp.float32)
         for j in range(q_columns // HD):
             lanes = slice(j * HD, (j + 1) * HD)
-            qown[at(c), lanes] = (total[:, lanes] * (scale * factor)).astype(jnp.bfloat16)
+            asked = (total[:, lanes] * (scale * factor)).astype(jnp.bfloat16)
+            qown[at(c), lanes] = asked
+            asked = asked.astype(jnp.float32)
+            query_norm = jnp.maximum(query_norm, jnp.sum(asked * asked, axis=1, keepdims=True))
 
         @pl.when(c >= chunks // 2)
         def _():
@@ -339,8 +343,39 @@
         def _():
             trade(c).start()
 
-        kv_out[e % 2, keys(s, c)] = (total[:, q_columns:] * scale).astype(jnp.bfloat16)
+        held = (total[:, q_columns:] * scale).astype(jnp.bfloat16)
+        kv_out[e % 2, keys(s, c)] = held
         pair(c).start()
+        held = held.astype(jnp.float32)
+        key_norm = jnp.sum(held * held, axis=1, keepdims=True) * (1 - e % 2).astype(jnp.float32)
+        for i, norm in enumerate((query_norm, key_norm)):
+            wide = jnp.broadcast_to(norm, (CHUNK, HD)).reshape(CHUNK // 8, 8, HD)
+            peak[0, i] = jnp.maximum(peak[0, i], jnp.max(wide, axis=0))
+
+    def meet(step, k):
+        goal = ((s, across(k)), (s, along(k)), ((s + k) % seq_count, e))[step]
+        return send(
+            peak.at[step], peaks.at[step, k], m_s.at[step, k], m_r.at[step, k], goal[0], goal[1]
+        )
+
+    sizes = (side, side, seq_count)
+
+    def climb(step, c):
+        @pl.when(c == chunks - 1)
+        def _():
+            if step > 0:
+                highest = peak[step - 1]
+                for k in range(1, sizes[step - 1]):
+                    meet(step - 1, k).wait_recv()
+                    highest = jnp.maximum(highest, peaks[step - 1, k])
+                if step < len(sizes):
+                    peak[step] = highest
+                else:
+                    bound = jnp.max(highest[0]) * jnp.max(highest[1])
+                    safe_out[0] = jnp.where(bound < SAFE * SAFE, 1, 0).astype(jnp.int32)
+            if step < len(sizes):
+                for k in range(1, sizes[step]):
+                    meet(step, k).start()
 
     def spread_out(c):
         pair(c).wait_recv()
@@ -353,8 +388,13 @@
             column(k, c).wait_recv()
             chip(k, c).start()
 
-    stages = (push, hop, multiply, merge, finish, spread_out, hand_over)
-    lags = (0, 2, 3, 4, 5, 6, 8)
+    climbs = [functools.partial(climb, step) for step in range(len(sizes) + 1)]
+    stages = (
+        push, hop, multiply, merge, finish, climbs[0], spread_out, climbs[1], climbs[2],
+        hand_over, climbs[3],
+    )
+    lags = (0, 2, 3, 4, 5, 5, 6, 6, 7, 8, 8)
+    peak[...] = jnp.zeros_like(peak)
 
     @pl.loop(0, chunks + lags[-1])
     def _(t):
@@ -382,6 +422,10 @@
     def _(c):
         trade(c).wait()
 
+    for step, size in enumerate(sizes):
+        for k in range(1, size):
+            meet(step, k).wait_send()
+
     @pl.loop(1, side)
     def _(k):
         weigh(k).wait_send()
@@ -416,11 +460,14 @@
             jax.ShapeDtypeStruct((rows, q_columns), bf16),
             jax.ShapeDtypeStruct((2, rows * seq_count, HD), bf16),
             jax.ShapeDtypeStruct((rows, HD), f32),
+            jax.ShapeDtypeStruct((1,), jnp.int32),
         ),
         in_specs=[pl.BlockSpec(memory_space=pltpu.SMEM)] * 2
         + [pl.BlockSpec(memory_space=VMEM), pl.BlockSpec(memory_space=pl.ANY)]
         + [pl.BlockSpec(memory_space=VMEM)] * 3,
-        out_specs=tuple([pl.BlockSpec(memory_space=VMEM)] * 3),
+        out_specs=tuple(
+            [pl.BlockSpec(memory_space=VMEM)] * 3 + [pl.BlockSpec(memory_space=pltpu.SMEM)]
+        ),
         scratch_shapes=[
             pltpu.SMEM((seq_count,), jnp.int32),
             VMEM((side, features, side * columns), bf16),
@@ -437,6 +484,8 @@
             VMEM((chunks, 8, CHUNK), f32),
             VMEM((side, chunks, 8, CHUNK), f32),
             VMEM((rows, q_columns), bf16),
+            VMEM((3, 2, 8, HD), f32),
+            VMEM((3, seq_count, 2, 8, HD), f32),
             *dma(enc_count),
             *dma(seq_count),
             *dma(side),
@@ -450,6 +499,7 @@
             *dma(ys, chunks),
             *dma(ys, chunks),
             *dma(chunks),
+            *dma(3, seq_count),
         ],
         compiler_params=pltpu.CompilerParams(
             collective_id=0, has_side_effects=True, vmem_limit_bytes=60 << 20
@@ -457,164 +507,191 @@
     )(image_count, text_gap, text, visual, gain, w_query, w_keyval)
 
 
-def attention_kernel(bq, bk, sbq, sbk, off_ref, q_ref, kv_ref, lim_ref, o_ref, acc, den, top):
+def masked_scores(q, keys, lim, key):
+    s = lax.dot_general(q, keys, (((1,), (1,)), ((), ())), preferred_element_type=jnp.float32)
+    if lim is None:
+        return s
+    at = (key + lax.broadcasted_iota(jnp.int32, s.shape, 1)).astype(jnp.float32)
+    return jnp.where(at <= jnp.concatenate([lim] * (s.shape[1] // HD), axis=1), s, NEG)
+
+
+def lane_sums(p):
+    total = p[:, :HD]
+    for part in range(1, p.shape[1] // HD):
+        total = total + p[:, part * HD : (part + 1) * HD]
+    return total
+
+
+def quick_kernel(bk, q_ref, kv_ref, lim_ref, o_ref, kv, lent, acc, den, kv_s, o_s, o_r):
+    s, e = lax.axis_index("seq"), lax.axis_index("enc")
+    seq_count = lax.axis_size("seq")
+    other = seq_count - 1 - s
     heads = q_ref.shape[1] // HD
-    rows_all, keys_all = q_ref.shape[0], kv_ref.shape[1]
-    q0 = off_ref[0]
-
-    def query_norm(step, best):
-        block = q_ref[pl.ds(pl.multiple_of(step * 128, 128), 128), :].astype(jnp.float32)
-        square = block * block
-        for head in range(heads):
-            norm = jnp.sum(square[:, head * HD : (head + 1) * HD], axis=1, keepdims=True)
-            best = jnp.maximum(best, norm)
-        return best
-
-    ones = jnp.ones((HD, HD), jnp.bfloat16)
-
-    def key_norm(step, best):
-        block = kv_ref[0, pl.ds(pl.multiple_of(step * bk, bk), bk), :]
-        norm = jnp.dot(block * block, ones, preferred_element_type=jnp.float32)
-        return jnp.maximum(best, jnp.max(norm.reshape(bk // 8, 8, HD), axis=0))
-
-    zero = jnp.zeros((128, 1), jnp.float32)
-    largest_query = jnp.max(lax.fori_loop(0, rows_all // 128, query_norm, zero))
-    largest_key = jnp.max(lax.fori_loop(0, keys_all // bk, key_norm, jnp.zeros((8, HD), jnp.float32)))
-    safe = largest_query * largest_key * 1.02 < SAFE * SAFE
-
-    def scores(row, head, size, key, count, masked):
-        q = q_ref[pl.ds(row, size), head * HD : (head + 1) * HD]
-        s = lax.dot_general(
-            q,
-            kv_ref[0, pl.ds(key, count), :],
-            (((1,), (1,)), ((), ())),
-            preferred_element_type=jnp.float32,
-        )
-        if masked:
-            at = (key + lax.broadcasted_iota(jnp.int32, (size, count), 1)).astype(jnp.float32)
-            lim = jnp.concatenate([lim_ref[pl.ds(row, size), :]] * (count // HD), axis=1)
-            s = jnp.where(at <= lim, s, NEG)
-        return s
-
-    def lane_sums(p):
-        total = p[:, :HD]
-        for part in range(1, p.shape[1] // HD):
-            total = total + p[:, part * HD : (part + 1) * HD]
-        return total
-
-    def tiles(size, count, begin, step, end):
-        @pl.loop(0, rows_all // size)
-        def _(tile):
-            row = pl.multiple_of(tile * size, size)
-            begin()
-            first = q0 + row
-            whole = first // count
-            last = jnp.minimum(pl.cdiv(first + size + 255, count), keys_all // count)
-
-            @pl.loop(0, whole)
-            def _(j):
-                step(row, pl.multiple_of(j * count, count), False)
-
-            @pl.loop(whole, last)
-            def _(j):
-                step(row, pl.multiple_of(j * count, count), True)
-
-            end(row)
-
-    @pl.when(safe)
-    def _():
-        def begin():
-            acc[...] = jnp.zeros_like(acc)
-            den[...] = jnp.zeros_like(den)
-
-        def step(row, key, masked):
-            values = kv_ref[1, pl.ds(key, bk), :]
+    rows = q_ref.shape[0]
+    half = rows // 2
+    blocks = kv_ref.shape[1] // bk
+
+    def load(j):
+        here = pl.ds(pl.multiple_of(j * bk, bk), bk)
+        return pltpu.make_async_copy(kv_ref.at[:, here], kv.at[:, here], kv_s.at[j])
+
+    @pl.loop(0, blocks)
+    def _(j):
+        load(j).start()
+
+    barrier = pltpu.get_barrier_semaphore()
+    pl.semaphore_signal(barrier, inc=1, device_id=(other, e), device_id_type=MESH)
+
+    def job(part, first, ready, target, base):
+        size = half
+        rows_here = pl.ds(part * half, half)
+        acc[...] = jnp.zeros_like(acc)
+        den[...] = jnp.zeros_like(den)
+        whole = first // bk
+        last = jnp.minimum((first + size + 255 + bk - 1) // bk, blocks)
+
+        def step(j, masked):
+            @pl.when(j >= ready)
+            def _():
+                load(j).wait()
+
+            key = pl.multiple_of(j * bk, bk)
+            keys, values = kv[0, pl.ds(key, bk), :], kv[1, pl.ds(key, bk), :]
+            lim = lim_ref[rows_here, :] if masked else None
             for head in range(heads):
-                p = jnp.exp2(scores(row, head, bq, key, bk, masked))
+                q = q_ref[rows_here, head * HD : (head + 1) * HD]
+                p = jnp.exp2(masked_scores(q, keys, lim, key))
                 acc[head] += jnp.dot(
                     p.astype(jnp.bfloat16), values, preferred_element_type=jnp.float32
                 )
                 den[head] += lane_sums(p)
 
-        def end(row):
+        @pl.loop(0, whole)
+        def _(j):
+            step(j, False)
+
+        @pl.loop(whole, last)
+        def _(j):
+            step(j, True)
+
+        for head in range(heads):
+            result = acc[head] / jnp.sum(den[head], axis=1, keepdims=True)
+            target[base : base + half, head * HD : (head + 1) * HD] = result.astype(jnp.bfloat16)
+        return last
+
+    used = job(0, other * rows, 0, lent, 0)
+    pl.semaphore_wait(barrier, 1)
+    back = pltpu.make_async_remote_copy(
+        src_ref=lent, dst_ref=o_ref.at[pl.ds(0, half)], send_sem=o_s, recv_sem=o_r,
+        device_id=(other, e), device_id_type=MESH,
+    )
+    back.start()
+    used = jnp.maximum(used, job(1, s * rows + half, used, o_ref, half))
+
+    @pl.loop(used, blocks)
+    def _(j):
+        load(j).wait()
+
+    back.wait()
+
+
+def quick(query, keyval, lim):
+    rows, width = query.shape
+    heads, bk = width // HD, 1024
+    return pl.pallas_call(
+        functools.partial(quick_kernel, bk),
+        out_shape=jax.ShapeDtypeStruct((rows, width), jnp.bfloat16),
+        in_specs=[
+            pl.BlockSpec(memory_space=VMEM),
+            pl.BlockSpec(memory_space=pl.ANY),
+            pl.BlockSpec(memory_space=VMEM),
+        ],
+        out_specs=pl.BlockSpec(memory_space=VMEM),
+        scratch_shapes=[
+            VMEM(keyval.shape, jnp.bfloat16),
+            VMEM((rows // 2, width), jnp.bfloat16),
+            VMEM((heads, rows // 2, HD), jnp.float32),
+            VMEM((heads, rows // 2, HD), jnp.float32),
+            pltpu.SemaphoreType.DMA((keyval.shape[1] // bk,)),
+            pltpu.SemaphoreType.DMA,
+            pltpu.SemaphoreType.DMA,
+        ],
+        compiler_params=pltpu.CompilerParams(
+            collective_id=1, has_side_effects=True, vmem_limit_bytes=56 << 20
+        ),
+    )(query, keyval, lim)
+
+
+def careful_kernel(bq, bk, off_ref, q_ref, kv_ref, lim_ref, o_ref, acc, den, top):
+    heads = q_ref.shape[1] // HD
+
+    @pl.loop(0, q_ref.shape[0] // bq)
+    def _(tile):
+        row = pl.multiple_of(tile * bq, bq)
+        acc[...] = jnp.zeros_like(acc)
+        den[...] = jnp.zeros_like(den)
+        top[...] = jnp.full_like(top, NEG)
+        last = jnp.minimum(pl.cdiv(off_ref[0] + row + bq + 255, bk), kv_ref.shape[1] // bk)
+
+        @pl.loop(0, last)
+        def _(j):
+            key = pl.multiple_of(j * bk, bk)
+            keys, values = kv_ref[0, pl.ds(key, bk), :], kv_ref[1, pl.ds(key, bk), :]
             for head in range(heads):
-                result = acc[head] / jnp.sum(den[head], axis=1, keepdims=True)
-                o_ref[pl.ds(row, bq), head * HD : (head + 1) * HD] = result.astype(jnp.bfloat16)
-
-        tiles(bq, bk, begin, step, end)
-
-    @pl.when(jnp.logical_not(safe))
-    def _():
-        part = pl.ds(0, sbq)
-
-        def begin():
-            acc[...] = jnp.zeros_like(acc)
-            den[...] = jnp.zeros_like(den)
-            top[...] = jnp.full_like(top, NEG)
-
-        def step(row, key, masked):
-            values = kv_ref[1, pl.ds(key, sbk), :]
-            for head in range(heads):
-                s = scores(row, head, sbq, key, sbk, masked)
+                q = q_ref[pl.ds(row, bq), head * HD : (head + 1) * HD]
+                s = masked_scores(q, keys, lim_ref[pl.ds(row, bq), :], key)
                 old = top[head]
                 new = jnp.maximum(old, jnp.max(s, axis=1, keepdims=True))
                 top[head] = new
                 p = jnp.exp2(s - new)
                 shrink = jnp.exp2(old - new)
-                acc[head, part] = acc[head, part] * shrink + jnp.dot(
+                acc[head] = acc[head] * shrink + jnp.dot(
                     p.astype(jnp.bfloat16), values, preferred_element_type=jnp.float32
                 )
-                den[head, part] = den[head, part] * shrink + lane_sums(p)
-
-        def end(row):
-            for head in range(heads):
-                result = acc[head, part] / jnp.sum(den[head, part], axis=1, keepdims=True)
-                o_ref[pl.ds(row, sbq), head * HD : (head + 1) * HD] = result.astype(jnp.bfloat16)
-
-        tiles(sbq, sbk, begin, step, end)
-
-
-def attention(q0, query, keyval, lim, part):
-    rows, width = query.shape[0] // 2, query.shape[1]
-    heads = width // HD
-    bq, bk, sbq, sbk = rows, 1024, 128, 512
-    flops = 4 * rows * keyval.shape[1] * width
-    return pl.pallas_call(
-        functools.partial(attention_kernel, bq, bk, sbq, sbk),
-        out_shape=jax.ShapeDtypeStruct((rows, width), jnp.bfloat16),
-        grid=(1,),
-        in_specs=[
-            pl.BlockSpec(memory_space=pltpu.SMEM),
-            pl.BlockSpec((rows, width), lambda i: (part, 0)),
-            pl.BlockSpec(memory_space=VMEM),
-            pl.BlockSpec((rows, HD), lambda i: (part, 0)),
-        ],
-        out_specs=pl.BlockSpec(memory_space=VMEM),
-        scratch_shapes=[
-            VMEM((heads, bq, HD), jnp.float32),
-            VMEM((heads, bq, HD), jnp.float32),
-            VMEM((heads, sbq, 1), jnp.float32),
-        ],
-        compiler_params=pltpu.CompilerParams(vmem_limit_bytes=56 << 20),
-        cost_estimate=pl.CostEstimate(
-            flops=flops, bytes_accessed=keyval.size * 2, transcendentals=rows * keyval.shape[1]
-        ),
-    )(q0, query, keyval, lim)
-
-
-def per_device(text, visual, gain, w_query, w_keyval, image_count, text_gap):
-    rows = text.shape[0]
-    query, keyval, lim = project(
-        text, visual, gain, w_query, w_keyval, image_count, text_gap
-    )
-    half = rows // 2
+                den[head] = den[head] * shrink + lane_sums(p)
+
+        for head in range(heads):
+            result = acc[head] / jnp.sum(den[head], axis=1, keepdims=True)
+            o_ref[pl.ds(row, bq), head * HD : (head + 1) * HD] = result.astype(jnp.bfloat16)
+
+
+def careful(query, keyval, lim):
+    rows, width = query.shape
+    half, heads, bq, bk = rows // 2, width // HD, 128, 512
     seq_count = lax.axis_size("seq")
     mine = (lax.axis_index("seq") * rows).astype(jnp.int32)
     theirs = (seq_count - 1) * rows - mine
-    lent = attention(theirs.reshape(1), query, keyval, lim, 0)
+
+    def attend(q0, part):
+        return pl.pallas_call(
+            functools.partial(careful_kernel, bq, bk),
+            out_shape=jax.ShapeDtypeStruct((half, width), jnp.bfloat16),
+            grid=(1,),
+            in_specs=[
+                pl.BlockSpec(memory_space=pltpu.SMEM),
+                pl.BlockSpec((half, width), lambda i: (part, 0)),
+                pl.BlockSpec(memory_space=VMEM),
+                pl.BlockSpec((half, HD), lambda i: (part, 0)),
+            ],
+            out_specs=pl.BlockSpec(memory_space=VMEM),
+            scratch_shapes=[
+                VMEM((heads, bq, HD), jnp.float32),
+                VMEM((heads, bq, HD), jnp.float32),
+                VMEM((heads, bq, 1), jnp.float32),
+            ],
+            compiler_params=pltpu.CompilerParams(vmem_limit_bytes=56 << 20),
+        )(q0.reshape(1), query, keyval, lim)
+
+    lent = attend(theirs, 0)
     back = lax.ppermute(lent, "seq", [(i, seq_count - 1 - i) for i in range(seq_count)])
-    own = attention((mine + half).reshape(1), query, keyval, lim, 1)
-    return jnp.concatenate((back, own), axis=0)
+    return jnp.concatenate((back, attend(mine + half, 1)), axis=0)
+
+
+def per_device(text, visual, gain, w_query, w_keyval, image_count, text_gap):
+    query, keyval, lim, safe = project(
+        text, visual, gain, w_query, w_keyval, image_count, text_gap
+    )
+    return lax.cond(safe[0] > 0, quick, careful, query, keyval, lim)
 
 
 def solution(mesh):

time: 275 us -> 273 us (level)
  Pallas kernels: 200 us -> 197 us
    pallas_call x2, Pallas kernels: 101 us -> 94.9 us  [attend(): pl.pallas_call(functools.partial(careful_kernel, bq, bk), out_shape=jax.S...]
    pallas_call x1, Pallas kernels: 98.5 us -> 102 us  [project(): pl.pallas_call(functools.partial(project_kernel, side), out_shape=(jax.Sh...]
  transfers between devices with their start and end apart: 1 -> 1, of which waited for: 0 -> 0; matrix products, arithmetic and copies ran while one was open for 0% -> 0% of each run, Pallas kernels for 32% -> 31%
where the time goes in v4:
time: 273 us
  Pallas kernels  197 us (72%)
  starting transfers between devices  73.7 us (27%)
    pallas_call x1, Pallas kernels, project(): pl.pallas_call(functools.partial(project_kernel, side), out_shape=(jax.Sh...  102 us
    pallas_call x2, Pallas kernels, attend(): pl.pallas_call(functools.partial(careful_kernel, bq, bk), out_shape=jax.S...  94.9 us
    ppermute x1, starting transfers between devices, careful(): lax.ppermute(lent, 'seq', [(i, seq_count - 1 - i) for i in range(seq_coun...  73.7 us
  transfers between devices with their start and end apart: 1, of which 0 were waited for; matrix products, arithmetic and copies ran while one was open for 0% of the time, Pallas kernels for 31%

profile of v4, /device:TPU:25, one launch (start us, length us, event | category | flops | bytes accessed | tf_op | source)
XLA Modules:
  0.0 273.0 jit_solution(17286640545118224034)
XLA Ops:
  0.0 102.0 %shard_map.75 = (bf16[1280,256]{1,0:T(8,128)(2,1)S(1)}, bf16[2,10240,128]{2,1,0:T(8,128)(2,1)}, f32[1280,128]{1,0:T(8,128)S(1)}, s32[1]{0:T(128)}) custom-call(s32[32]{0:T(128)} %count_ref.1, s32[33]{0:T(128)} %gap_ref.1, bf16[1280,256]{1,0:T(8,128)(2,1)} %text_ref.1, bf16[40,4096]{1,0:T(8,128)(2,1)} %visual_ref.1, bf16[256]{0:T(256)(128)(2,1)} %gain_ref.1, ...), custom_call_target="tpu_custom_call" | custom-call | tf_op jit(solution)/shard_map/pallas_call | solution.py:457
  102.6 169.6 %conditional.1 = (bf16[1280,256]{1,0:T(8,128)(2,1)S(1)}) conditional(s32[]{:T(128)} %bitcast.2, (bf16[1280,256]{1,0:T(8,128)(2,1)S(1)}, bf16[2,10240,128]{2,1,0:T(8,128)(2,1)}, f32[1280,128]{1,0:T(8,128)S(1)}) %tuple.11, (bf16[1280,256]{1,0:T(8,128)(2,1)S(1)}, bf16[2,10240,128]{2,1,0:T(8,128)(2,1)}, f32[1280,128]{1,0:T(8,128)S(1)}) %tuple.11), branch_computations={%region_0.0_spmd, %region_1.0_spmd} | conditional | flops 1310726 | bytes 2621556 | solution.py:694
  102.6 10.4 %branch_0_fun.2 = bf16[640,256]{1,0:T(8,128)(2,1)} custom-call(s32[1]{0:T(128)} %bitcast.off_ref, bf16[1280,256]{1,0:T(8,128)(2,1)S(1)} %get-tuple-element.20.q_ref, bf16[2,10240,128]{2,1,0:T(8,128)(2,1)} %get-tuple-element.21.kv_ref, f32[1280,128]{1,0:T(8,128)S(1)} %get-tuple-element.22.lim_ref), custom_call_target="tpu_custom_call" | custom-call | tf_op jit(solution)/shard_map/cond/branch_0_fun/pallas_call | solution.py:666
  113.0 73.7 %collective-permute-start = (bf16[640,256]{1,0:T(8,128)(2,1)}, bf16[640,256]{1,0:T(8,128)(2,1)S(1)}, u32[]{:S(2)}, u32[]{:S(2)}) collective-permute-start(bf16[640,256]{1,0:T(8,128)(2,1)} %branch_0_fun.2), channel_id=1, source_target_pairs={{0,112},{16,96},{32,80},{48,64},{64,48},{80,32},{96,16},{112,0},{1... | collective-permute-start | bytes 983048 | tf_op jit(solution)/shard_map/cond/branch_0_fun/ppermute | solution.py:686
  186.6 84.5 %branch_0_fun.3 = bf16[640,256]{1,0:T(8,128)(2,1)} custom-call(s32[1]{0:T(128)} %bitcast.1.off_ref, bf16[1280,256]{1,0:T(8,128)(2,1)S(1)} %get-tuple-element.20.q_ref, bf16[2,10240,128]{2,1,0:T(8,128)(2,1)} %get-tuple-element.21.kv_ref, f32[1280,128]{1,0:T(8,128)S(1)} %get-tuple-element.22.lim_ref), custom_call_target="tpu_custom_call" | custom-call | tf_op jit(solution)/shard_map/cond/branch_0_fun/pallas_call | solution.py:666
  271.2 0.0 collective-permute-done
  271.2 1.0 pad_maximum_fusion
  272.2 0.8 copy.13
Async XLA Ops:
  113.0 158.2 %collective-permute-start = (bf16[640,256]{1,0:T(8,128)(2,1)}, bf16[640,256]{1,0:T(8,128)(2,1)S(1)}, u32[]{:S(2)}, u32[]{:S(2)}) collective-permute-start(bf16[640,256]{1,0:T(8,128)(2,1)} %branch_0_fun.2), channel_id=1, source_target_pairs={{0,112},{16,96},{32,80},{48,64},{64,48},{80,32},{96,16},{112,0},{1... | collective-permute-start | bytes 983048 | tf_op jit(solution)/shard_map/cond/branch_0_fun/ppermute | solution.py:686

commit v5 on v4

--- a/solution.py
+++ b/solution.py
@@ -11,6 +11,7 @@
 HD = 128
 EPS = 1e-05
 CHUNK = 128
+LAG = 1
 MESH = pl.DeviceIdType.MESH
 NEG = -1e30
 SAFE = 64.0
@@ -23,11 +24,11 @@
 
 def project_kernel(
     side, count_ref, gap_ref, text_ref, visual_ref, gain_ref, wq_ref, wkv_ref,
-    q_out, kv_out, lim_out, safe_out,
-    before, wsend, wall, seen, picked, landed, slots, lims, xall, psend, pmid, precv, squares,
-    sqrecv, qown, peak, peaks,
-    vis_s, vis_r, blk_s, blk_r, w_s, w_r, wf_s, wf_r, x_s, x_r, xf_s, xf_r, p_s, p_r, pf_s, pf_r,
-    n_s, n_r, kx_s, kx_r, ky_s, ky_r, kc_s, kc_r, q_s, q_r, m_s, m_r,
+    q_out, kv_out, lim_out, peak,
+    before, scales, wsend, wall, seen, picked, landed, slots, lims, xall, psend_k, psend_q, pmid_k,
+    pmid_q, precv_k, precv_q, squares, sqrecv, factors, qown,
+    vis_s, vis_r, blk_s, blk_r, w_s, w_r, wp_s, wp_r, wr_s, wr_r, x_s, x_r, xf_s, xf_r, p_s, p_r, pf_s, pf_r,
+    n_s, n_r, kx_s, kx_r, ky_s, ky_r, kc_s, kc_r, q_s, q_r,
 ):
     seq_count, enc_count = lax.axis_size("seq"), lax.axis_size("enc")
     s, e = lax.axis_index("seq"), lax.axis_index("enc")
@@ -37,10 +38,10 @@
     chunks = rows // CHUNK
     window = landed.shape[1]
     vis_rows = seen.shape[1]
-    columns = psend.shape[2]
-    q_columns = q_out.shape[1]
-    k_columns = columns - q_columns
-    half = wall.shape[2] // 2
+    q_columns, k_columns = psend_q.shape[2], psend_k.shape[2]
+    psend, pmid, precv = (psend_k, psend_q), (pmid_k, pmid_q), (precv_k, precv_q)
+    split = side * k_columns
+    KEYS, QUERIES = 0, 1
     images = count_ref.shape[0]
     twin = s + 1 - 2 * core
     mate = e + 1 - 2 * (e % 2)
@@ -81,9 +82,66 @@
         there = seen.at[e, pl.ds(0, visual_ref.shape[0])]
         return send(visual_ref.at[:, lanes], there, vis_s.at[k], vis_r.at[k], s, to)
 
+    for g in range(features // HD):
+        scales[g * HD : (g + 1) * HD, :] = spread(
+            gain_ref[g * HD : (g + 1) * HD].astype(jnp.float32).reshape(1, HD)
+        )
+
+    def scaled(ref, here, start):
+        lanes = pl.ds(pl.multiple_of(start, HD), HD)
+        return (ref[here, lanes].astype(jnp.float32) * scales[here, :]).astype(jnp.bfloat16)
+
+    def gather_columns(target, here, to):
+        for zz in range(side):
+            owner = zz * side + to
+            for j in range(q_columns // HD):
+                target[:, pl.ds(split + zz * q_columns + j * HD, HD)] = scaled(
+                    wq_ref, here, owner * q_columns + j * HD
+                )
+            for j in range(k_columns // HD):
+                target[:, pl.ds(zz * k_columns + j * HD, HD)] = scaled(
+                    wkv_ref, here, owner * k_columns + j * HD
+                )
+
+    deep = features // seq_count
+
+    def part_of(owner):
+        return pl.ds(pl.multiple_of(owner * deep, deep), deep)
+
+    def weigh(k):
+        return send(
+            wsend.at[(x + k) % side], wall.at[x, part_of(s)], w_s.at[k], w_r.at[k], s, across(k)
+        )
+
+    def pass_weights(k, j):
+        here = wall.at[(x + side - k) % side, part_of(s)]
+        goal = twin if j == 0 else column_of(j)
+        return send(here, here, wp_s.at[k, j], wp_r.at[k, j], goal, e)
+
+    def relay_weights(k, j):
+        here = wall.at[(x + side - k) % side, part_of(column_of(ys - j))]
+        return send(here, here, wr_s.at[k, j], wr_r.at[k, j], twin, e)
+
+    def pass_all(k):
+        weigh(k).wait_recv()
+        for j in range(1, ys):
+            pass_weights(k, j).start()
+        pass_weights(k, 0).start()
+
+    @pl.loop(1, side)
+    def _(k):
+        to = (x + k) % side
+        gather_columns(wsend.at[to], part_of(s), to)
+
+    for k in sides:
+        weigh(k).start()
+
     @pl.loop(1, enc_count)
     def _(k):
         see(k).start()
+
+    for k in range(2, side - 1):
+        weigh(k).start()
 
     kept = pltpu.make_async_copy(
         visual_ref.at[:, pl.ds(pl.multiple_of(e * features, features), features)],
@@ -92,49 +150,8 @@
     )
     kept.start()
 
-    gains = [
-        spread(gain_ref[g * HD : (g + 1) * HD].astype(jnp.float32).reshape(1, HD)) for g in range(features // HD)
-    ]
-
-    def scaled(ref, part, start):
-        lanes = pl.ds(pl.multiple_of(start, HD), HD)
-        block = ref[part * HD : (part + 1) * HD, lanes].astype(jnp.float32)
-        return (block * gains[part]).astype(jnp.bfloat16)
-
-    @pl.loop(0, side)
-    def _(to):
-        for zz in range(side):
-            for part in range(features // HD):
-                there = pl.ds(part * HD, HD)
-                owner = zz * side + to
-                for j in range(q_columns // HD):
-                    wsend[to, there, pl.ds(zz * columns + j * HD, HD)] = scaled(
-                        wq_ref, part, owner * q_columns + j * HD
-                    )
-                for j in range(k_columns // HD):
-                    wsend[to, there, pl.ds(zz * columns + q_columns + j * HD, HD)] = scaled(
-                        wkv_ref, part, owner * k_columns + j * HD
-                    )
-
-    mine = pl.ds(pl.multiple_of(core * half, HD), half)
-
-    def weigh(k):
-        return send(
-            wsend.at[(x + k) % side, :, mine], wall.at[x, :, mine],
-            w_s.at[k], w_r.at[k], s, across(k),
-        )
-
-    def pass_weights(k):
-        origin = (x + side - k) % side
-        return send(
-            wall.at[origin, :, mine], wall.at[origin, :, mine], wf_s.at[k], wf_r.at[k], twin, e
-        )
-
-    @pl.loop(1, side)
-    def _(k):
-        weigh(k).start()
-
-    wall[x] = wsend[x]
+    for g in range(features // HD):
+        gather_columns(wall.at[x, pl.ds(g * HD, HD)], pl.ds(g * HD, HD), x)
 
     shape = slots.shape
     position = (
@@ -177,6 +194,9 @@
     slot = origin * window + (token // group) * enc_count + token % enc_count - skipped
     slots[...] = jnp.where(shift <= 0, slot, -1).astype(jnp.float32)
 
+    for k in sides:
+        pass_all(k)
+
     @pl.loop(1, enc_count)
     def _(k):
         see(k).wait_recv()
@@ -211,10 +231,8 @@
 
     landed[s] = pick(s)
 
-    @pl.loop(1, side)
-    def _(k):
-        weigh(k).wait_recv()
-        pass_weights(k).start()
+    for k in range(2, side - 1):
+        pass_all(k)
 
     @pl.loop(1, seq_count)
     def _(k):
@@ -233,16 +251,16 @@
         here = xall.at[(x + side - k) % side, half_of(k, c)]
         return send(here, here, xf_s.at[k, c], xf_r.at[k, c], s, across(k))
 
-    def reach(k, c):
+    def reach(kind, k, c):
         return send(
-            psend.at[(z + side // 2) % side, half_of(k, c)], pmid.at[half_of(k, c)],
-            pf_s.at[k, c], pf_r.at[k, c], s, along(k),
-        )
-
-    def reduce(k, c):
+            psend[kind].at[(z + side // 2) % side, half_of(k, c)], pmid[kind].at[half_of(k, c)],
+            pf_s.at[kind, k, c], pf_r.at[kind, k, c], s, along(k),
+        )
+
+    def reduce(kind, k, c):
         return send(
-            psend.at[(z + k) % side, at(c)], precv.at[k // 2, at(c)],
-            p_s.at[k, c], p_r.at[k, c], s, along(k),
+            psend[kind].at[(z + k) % side, at(c)], precv[kind].at[k // 2, at(c)],
+            p_s.at[kind, k, c], p_r.at[kind, k, c], s, along(k),
         )
 
     def trade(c):
@@ -288,7 +306,13 @@
         @pl.when(c == 0)
         def _():
             for k in range(1, side):
-                pass_weights(k).wait_recv()
+                for j in range(1, ys):
+                    pass_weights(k, j).wait_recv()
+                    relay_weights(k, j).start()
+            for k in range(1, side):
+                pass_weights(k, 0).wait_recv()
+                for j in range(1, ys):
+                    relay_weights(k, j).wait_recv()
 
         for k in sides:
             relay(k, c).wait_recv()
@@ -300,40 +324,65 @@
         )
         for k in range(1, side):
             norms(k, c).start()
-        weights = wall[...].reshape(side * features, side * columns)
+        launch(KEYS, c, block, 0, split)
+
+    def launch(kind, c, block, start, stop):
+        weights = wall[:, :, start:stop].reshape(side * features, stop - start)
         partial = jnp.dot(block, weights, preferred_element_type=jnp.float32).astype(jnp.bfloat16)
+        width = (stop - start) // side
         for zz in range(side):
-            psend[zz, at(c)] = partial[:, zz * columns : (zz + 1) * columns]
+            psend[kind][zz, at(c)] = partial[:, zz * width : (zz + 1) * width]
         for k in sides:
-            reach(k, c).start()
-
-    def merge(c):
+            reach(kind, k, c).start()
+
+    def multiply_queries(c):
+        block = jnp.concatenate([xall[j, at(c)] for j in range(side)], axis=1)
+        launch(QUERIES, c, block, split, split + side * q_columns)
+
+    def merge(kind, c):
         for k in sides:
-            reach(k, c).wait_recv()
-            rows_here = half_of(k, c)
+            reach(kind, k, c).wait_recv()
+            here = half_of(k, c)
             target = (z + k) % side
-            joined = psend[target, rows_here].astype(jnp.float32) + pmid[rows_here].astype(jnp.float32)
-            psend[target, rows_here] = joined.astype(jnp.bfloat16)
-            reduce(k, c).start()
-
-    def finish(c):
-        total = psend[z, at(c)].astype(jnp.float32)
+            joined = psend[kind][target, here].astype(jnp.float32) + pmid[kind][here].astype(jnp.float32)
+            psend[kind][target, here] = joined.astype(jnp.bfloat16)
+            reduce(kind, k, c).start()
+
+    def total_of(kind, c):
+        total = psend[kind][z, at(c)].astype(jnp.float32)
+        for k in sides:
+            reduce(kind, k, c).wait_recv()
+            total = total + precv[kind][k // 2, at(c)].astype(jnp.float32)
+        return total
+
+    def record(i, norm):
+        wide = jnp.broadcast_to(norm, (CHUNK, HD)).reshape(CHUNK // 8, 8, HD)
+        peak[i] = jnp.maximum(peak[i], jnp.max(wide, axis=0))
+
+    def finish_keys(c):
+        total = total_of(KEYS, c)
         square = squares[c]
-        for k in sides:
-            reduce(k, c).wait_recv()
-            total = total + precv[k // 2, at(c)].astype(jnp.float32)
         for k in range(1, side):
             norms(k, c).wait_recv()
             square = square + sqrecv[k, c]
         scale = spread(lax.rsqrt(square / (features * enc_count) + EPS)[0:1, :])
-        factor = math.log2(math.e) / HD**0.5
-        query_norm = jnp.zeros((CHUNK, 1), jnp.float32)
+        factors[at(c), :] = scale * (math.log2(math.e) / HD**0.5)
+        held = (total * scale).astype(jnp.bfloat16)
+        kv_out[e % 2, keys(s, c)] = held
+        pair(c).start()
+        held = held.astype(jnp.float32)
+        norm = jnp.sum(held * held, axis=1, keepdims=True)
+        record(1, norm * (1 - e % 2).astype(jnp.float32))
+
+    def finish_queries(c):
+        total = total_of(QUERIES, c)
+        norm = jnp.zeros((CHUNK, 1), jnp.float32)
         for j in range(q_columns // HD):
             lanes = slice(j * HD, (j + 1) * HD)
-            asked = (total[:, lanes] * (scale * factor)).astype(jnp.bfloat16)
+            asked = (total[:, lanes] * factors[at(c), :]).astype(jnp.bfloat16)
             qown[at(c), lanes] = asked
             asked = asked.astype(jnp.float32)
-            query_norm = jnp.maximum(query_norm, jnp.sum(asked * asked, axis=1, keepdims=True))
+            norm = jnp.maximum(norm, jnp.sum(asked * asked, axis=1, keepdims=True))
 
         @pl.when(c >= chunks // 2)
         def _():
@@ -343,39 +392,7 @@
         def _():
             trade(c).start()
 
-        held = (total[:, q_columns:] * scale).astype(jnp.bfloat16)
-        kv_out[e % 2, keys(s, c)] = held
-        pair(c).start()
-        held = held.astype(jnp.float32)
-        key_norm = jnp.sum(held * held, axis=1, keepdims=True) * (1 - e % 2).astype(jnp.float32)
-        for i, norm in enumerate((query_norm, key_norm)):
-            wide = jnp.broadcast_to(norm, (CHUNK, HD)).reshape(CHUNK // 8, 8, HD)
-            peak[0, i] = jnp.maximum(peak[0, i], jnp.max(wide, axis=0))
-
-    def meet(step, k):
-        goal = ((s, across(k)), (s, along(k)), ((s + k) % seq_count, e))[step]
-        return send(
-            peak.at[step], peaks.at[step, k], m_s.at[step, k], m_r.at[step, k], goal[0], goal[1]
-        )
-
-    sizes = (side, side, seq_count)
-
-    def climb(step, c):
-        @pl.when(c == chunks - 1)
-        def _():
-            if step > 0:
-                highest = peak[step - 1]
-                for k in range(1, sizes[step - 1]):
-                    meet(step - 1, k).wait_recv()
-                    highest = jnp.maximum(highest, peaks[step - 1, k])
-                if step < len(sizes):
-                    peak[step] = highest
-                else:
-                    bound = jnp.max(highest[0]) * jnp.max(highest[1])
-                    safe_out[0] = jnp.where(bound < SAFE * SAFE, 1, 0).astype(jnp.int32)
-            if step < len(sizes):
-                for k in range(1, sizes[step]):
-                    meet(step, k).start()
+        record(0, norm)
 
     def spread_out(c):
         pair(c).wait_recv()
@@ -388,15 +405,15 @@
             column(k, c).wait_recv()
             chip(k, c).start()
 
-    climbs = [functools.partial(climb, step) for step in range(len(sizes) + 1)]
+    behind = LAG
     stages = (
-        push, hop, multiply, merge, finish, climbs[0], spread_out, climbs[1], climbs[2],
-        hand_over, climbs[3],
-    )
-    lags = (0, 2, 3, 4, 5, 5, 6, 6, 7, 8, 8)
+        push, hop, multiply, multiply_queries, functools.partial(merge, KEYS),
+        functools.partial(merge, QUERIES), finish_keys, spread_out, finish_queries, hand_over,
+    )
+    lags = (0, 2, 3, 3 + behind, 4, 4 + behind, 5, 6, 5 + behind, 8)
     peak[...] = jnp.zeros_like(peak)
 
-    @pl.loop(0, chunks + lags[-1])
+    @pl.loop(0, chunks + max(lags))
     def _(t):
         for stage, lag in zip(stages, lags):
             @pl.when((t >= lag) & (t < chunks + lag))
@@ -413,8 +430,9 @@
         for k in sides:
             share(k, c).wait_send()
             relay(k, c).wait_send()
-            reach(k, c).wait_send()
-            reduce(k, c).wait_send()
+            for kind in (KEYS, QUERIES):
+                reach(kind, k, c).wait_send()
+                reduce(kind, k, c).wait_send()
         for k in range(1, side):
             norms(k, c).wait_send()
 
@@ -422,14 +440,13 @@
     def _(c):
         trade(c).wait()
 
-    for step, size in enumerate(sizes):
-        for k in range(1, size):
-            meet(step, k).wait_send()
-
     @pl.loop(1, side)
     def _(k):
         weigh(k).wait_send()
-        pass_weights(k).wait_send()
+        for j in range(ys):
+            pass_weights(k, j).wait_send()
+        for j in range(1, ys):
+            relay_weights(k, j).wait_send()
 
     @pl.loop(1, enc_count)
     def _(k):
@@ -460,17 +477,16 @@
             jax.ShapeDtypeStruct((rows, q_columns), bf16),
             jax.ShapeDtypeStruct((2, rows * seq_count, HD), bf16),
             jax.ShapeDtypeStruct((rows, HD), f32),
-            jax.ShapeDtypeStruct((1,), jnp.int32),
+            jax.ShapeDtypeStruct((2, 8, HD), f32),
         ),
         in_specs=[pl.BlockSpec(memory_space=pltpu.SMEM)] * 2
         + [pl.BlockSpec(memory_space=VMEM), pl.BlockSpec(memory_space=pl.ANY)]
         + [pl.BlockSpec(memory_space=VMEM)] * 3,
-        out_specs=tuple(
-            [pl.BlockSpec(memory_space=VMEM)] * 3 + [pl.BlockSpec(memory_space=pltpu.SMEM)]
-        ),
+        out_specs=tuple([pl.BlockSpec(memory_space=VMEM)] * 4),
         scratch_shapes=[
             pltpu.SMEM((seq_count,), jnp.int32),
-            VMEM((side, features, side * columns), bf16),
+            VMEM((features, HD), f32),
+            VMEM((side, features // seq_count, side * columns), bf16),
             VMEM((side, features, side * columns), bf16),
             VMEM((enc_count, vis_rows, features), bf16),
             VMEM((seq_count, window, features), bf16),
@@ -478,28 +494,30 @@
             VMEM((16, HD), f32),
             VMEM((16, HD), f32),
             VMEM((side, rows, features), bf16),
-            VMEM((side, rows, columns), bf16),
-            VMEM((rows, columns), bf16),
-            VMEM((2, rows, columns), bf16),
+            VMEM((side, rows, columns - q_columns), bf16),
+            VMEM((side, rows, q_columns), bf16),
+            VMEM((rows, columns - q_columns), bf16),
+            VMEM((rows, q_columns), bf16),
+            VMEM((2, rows, columns - q_columns), bf16),
+            VMEM((2, rows, q_columns), bf16),
             VMEM((chunks, 8, CHUNK), f32),
             VMEM((side, chunks, 8, CHUNK), f32),
+            VMEM((rows, HD), f32),
             VMEM((rows, q_columns), bf16),
-            VMEM((3, 2, 8, HD), f32),
-            VMEM((3, seq_count, 2, 8, HD), f32),
             *dma(enc_count),
             *dma(seq_count),
             *dma(side),
-            *dma(side),
+            *dma(side, ys),
+            *dma(side, ys),
             *dma(side, chunks),
             *dma(side, chunks),
-            *dma(side, chunks),
-            *dma(side, chunks),
+            *dma(2, side, chunks),
+            *dma(2, side, chunks),
             *dma(side, chunks),
             *dma(chunks),
             *dma(ys, chunks),
             *dma(ys, chunks),
             *dma(chunks),
-            *dma(3, seq_count),
         ],
         compiler_params=pltpu.CompilerParams(
             collective_id=0, has_side_effects=True, vmem_limit_bytes=60 << 20
@@ -522,7 +540,10 @@
     return total
 
 
-def quick_kernel(bk, q_ref, kv_ref, lim_ref, o_ref, kv, lent, acc, den, kv_s, o_s, o_r):
+def quick_kernel(
+    bk, side, q_ref, kv_ref, lim_ref, top_ref, o_ref, safe_ref,
+    kv, lent, acc, den, peak, peaks, kv_s, o_s, o_r, m_s, m_r,
+):
     s, e = lax.axis_index("seq"), lax.axis_index("enc")
     seq_count = lax.axis_size("seq")
     other = seq_count - 1 - s
@@ -540,9 +561,43 @@
         load(j).start()
 
     barrier = pltpu.get_barrier_semaphore()
-    pl.semaphore_signal(barrier, inc=1, device_id=(other, e), device_id_type=MESH)
-
-    def job(part, first, ready, target, base):
+    z, x = e // side, e % side
+    sizes = (side, side, seq_count)
+
+    def goal(step, k):
+        if step == 0:
+            return s, z * side + (x + k) % side
+        if step == 1:
+            return s, ((z + k) % side) * side + x
+        return (s + k) % seq_count, e
+
+    for step, size in enumerate(sizes):
+        for k in range(1, size):
+            pl.semaphore_signal(barrier, inc=1, device_id=goal(step, k), device_id_type=MESH)
+
+    peak[0] = top_ref[...]
+
+    def meet(step, k):
+        return pltpu.make_async_remote_copy(
+            src_ref=peak.at[step], dst_ref=peaks.at[step, k], send_sem=m_s.at[step, k],
+            recv_sem=m_r.at[step, k], device_id=goal(step, k), device_id_type=MESH,
+        )
+
+    def climb(step):
+        if step > 0:
+            highest = peak[step - 1]
+            for k in range(1, sizes[step - 1]):
+                meet(step - 1, k).wait_recv()
+                highest = jnp.maximum(highest, peaks[step - 1, k])
+            if step == len(sizes):
+                bound = jnp.max(highest[0]) * jnp.max(highest[1])
+                safe_ref[0] = jnp.where(bound < SAFE * SAFE, 1, 0).astype(jnp.int32)
+                return
+            peak[step] = highest
+        for k in range(1, sizes[step]):
+            meet(step, k).start()
+
+    def job(part, first, ready, target, base, hook):
         size = half
         rows_here = pl.ds(part * half, half)
         acc[...] = jnp.zeros_like(acc)
@@ -570,56 +625,74 @@
         def _(j):
             step(j, False)
 
+        hook(1)
+
         @pl.loop(whole, last)
         def _(j):
             step(j, True)
 
+        hook(2)
         for head in range(heads):
             result = acc[head] / jnp.sum(den[head], axis=1, keepdims=True)
             target[base : base + half, head * HD : (head + 1) * HD] = result.astype(jnp.bfloat16)
         return last
 
-    used = job(0, other * rows, 0, lent, 0)
-    pl.semaphore_wait(barrier, 1)
+    used = job(0, other * rows, 0, lent, 0, lambda step: None)
+    pl.semaphore_wait(barrier, sum(sizes) - len(sizes))
     back = pltpu.make_async_remote_copy(
         src_ref=lent, dst_ref=o_ref.at[pl.ds(0, half)], send_sem=o_s, recv_sem=o_r,
         device_id=(other, e), device_id_type=MESH,
     )
     back.start()
-    used = jnp.maximum(used, job(1, s * rows + half, used, o_ref, half))
+    climb(0)
+    used = jnp.maximum(used, job(1, s * rows + half, used, o_ref, half, climb))
 
     @pl.loop(used, blocks)
     def _(j):
         load(j).wait()
 
+    climb(3)
     back.wait()
-
-
-def quick(query, keyval, lim):
+    for step, size in enumerate(sizes):
+        for k in range(1, size):
+            meet(step, k).wait_send()
+
+
+def quick(query, keyval, lim, peak):
     rows, width = query.shape
+    seq_count = lax.axis_size("seq")
+    side = math.isqrt(lax.axis_size("enc"))
     heads, bk = width // HD, 1024
     return pl.pallas_call(
-        functools.partial(quick_kernel, bk),
-        out_shape=jax.ShapeDtypeStruct((rows, width), jnp.bfloat16),
+        functools.partial(quick_kernel, bk, side),
+        out_shape=(
+            jax.ShapeDtypeStruct((rows, width), jnp.bfloat16),
+            jax.ShapeDtypeStruct((1,), jnp.int32),
+        ),
         in_specs=[
             pl.BlockSpec(memory_space=VMEM),
             pl.BlockSpec(memory_space=pl.ANY),
             pl.BlockSpec(memory_space=VMEM),
+            pl.BlockSpec(memory_space=VMEM),
         ],
-        out_specs=pl.BlockSpec(memory_space=VMEM),
+        out_specs=(pl.BlockSpec(memory_space=VMEM), pl.BlockSpec(memory_space=pltpu.SMEM)),
         scratch_shapes=[
             VMEM(keyval.shape, jnp.bfloat16),
             VMEM((rows // 2, width), jnp.bfloat16),
             VMEM((heads, rows // 2, HD), jnp.float32),
             VMEM((heads, rows // 2, HD), jnp.float32),
+            VMEM((3, 2, 8, HD), jnp.float32),
+            VMEM((3, seq_count, 2, 8, HD), jnp.float32),
             pltpu.SemaphoreType.DMA((keyval.shape[1] // bk,)),
             pltpu.SemaphoreType.DMA,
             pltpu.SemaphoreType.DMA,
+            pltpu.SemaphoreType.DMA((3, seq_count)),
+            pltpu.SemaphoreType.DMA((3, seq_count)),
         ],
         compiler_params=pltpu.CompilerParams(
             collective_id=1, has_side_effects=True, vmem_limit_bytes=56 << 20
         ),
-    )(query, keyval, lim)
+    )(query, keyval, lim, peak)
 
 
 def careful_kernel(bq, bk, off_ref, q_ref, kv_ref, lim_ref, o_ref, acc, den, top):
@@ -688,10 +761,16 @@
 
 
 def per_device(text, visual, gain, w_query, w_keyval, image_count, text_gap):
-    query, keyval, lim, safe = project(
+    query, keyval, lim, peak = project(
         text, visual, gain, w_query, w_keyval, image_count, text_gap
     )
-    return lax.cond(safe[0] > 0, quick, careful, query, keyval, lim)
+    attended, safe = quick(query, keyval, lim, peak)
+    return lax.cond(
+        safe[0] > 0,
+        lambda done, *rest: done,
+        lambda done, *rest: careful(*rest),
+        attended, query, keyval, lim,
+    )
 
 
 def solution(mesh):

time: 273 us -> 296 us (1.084)
  Pallas kernels: 197 us -> 223 us
    pallas_call x0 -> x1, Pallas kernels: none -> 29.6 us  [quick(): pl.pallas_call(functools.partial(quick_kernel, bk, side), out_shape=(jax....]
    pallas_call x1, Pallas kernels: 102 us -> 98 us  [project(): pl.pallas_call(functools.partial(project_kernel, side), out_shape=(jax.Sh...]
  transfers between devices with their start and end apart: 1 -> 1, of which waited for: 0 -> 0; matrix products, arithmetic and copies ran while one was open for 0% -> 0% of each run, Pallas kernels for 31% -> 29%
where the time goes in v5:
time: 296 us
  Pallas kernels  223 us (75%)
  starting transfers between devices  70.8 us (24%)
    pallas_call x1, Pallas kernels, project(): pl.pallas_call(functools.partial(project_kernel, side), out_shape=(jax.Sh...  98 us
    pallas_call x2, Pallas kernels, attend(): pl.pallas_call(functools.partial(careful_kernel, bq, bk), out_shape=jax.S...  94.9 us
    ppermute x1, starting transfers between devices, careful(): lax.ppermute(lent, 'seq', [(i, seq_count - 1 - i) for i in range(seq_coun...  70.8 us
    pallas_call x1, Pallas kernels, quick(): pl.pallas_call(functools.partial(quick_kernel, bk, side), out_shape=(jax....  29.6 us
  transfers between devices with their start and end apart: 1, of which 0 were waited for; matrix products, arithmetic and copies ran while one was open for 0% of the time, Pallas kernels for 29%

profile of v5, /device:TPU:25, one launch (start us, length us, event | category | flops | bytes accessed | tf_op | source)
XLA Modules:
  0.0 295.8 jit_solution(4358351306430607228)
XLA Ops:
  0.0 98.0 %shard_map.75 = (bf16[1280,256]{1,0:T(8,128)(2,1)S(1)}, bf16[2,10240,128]{2,1,0:T(8,128)(2,1)}, f32[1280,128]{1,0:T(8,128)S(1)}, f32[2,8,128]{2,1,0:T(8,128)}) custom-call(s32[32]{0:T(128)} %count_ref.1, s32[33]{0:T(128)} %gap_ref.1, bf16[1280,256]{1,0:T(8,128)(2,1)} %text_ref.1, bf16[40,4096]{1,0:T(8,128)(2,1)} %visual_ref.1, bf16[256]{0:T(256)(128)(2,1)} %gain_ref.1, ...), custom_call_target="tpu_custom_call" | custom-call | tf_op jit(solution)/shard_map/pallas_call | solution.py:474
  98.0 29.6 %shard_map.76 = (bf16[1280,256]{1,0:T(8,128)(2,1)S(1)}, s32[1]{0:T(128)}) custom-call(bf16[1280,256]{1,0:T(8,128)(2,1)S(1)} %get-tuple-element.24.q_ref, bf16[2,10240,128]{2,1,0:T(8,128)(2,1)} %get-tuple-element.25.kv_ref, f32[1280,128]{1,0:T(8,128)S(1)} %get-tuple-element.26.lim_ref, f32[2,8,128]{2,1,0:T(8,128)} %get-tuple-element.27.top_ref), custom_call_target="tpu_custom_call" | custom-call | tf_op jit(solution)/shard_map/pallas_call | solution.py:666
  128.2 166.7 %conditional.1 = (bf16[1280,256]{1,0:T(8,128)(2,1)S(1)}) conditional(s32[]{:T(128)} %bitcast.2, (bf16[1280,256]{1,0:T(8,128)(2,1)S(1)}, bf16[2,10240,128]{2,1,0:T(8,128)(2,1)}, f32[1280,128]{1,0:T(8,128)S(1)}) %tuple.11, bf16[1280,256]{1,0:T(8,128)(2,1)S(1)} %get-tuple-element.29), branch_computations={%region_0.0_spmd, %region_1.0_spmd} | conditional | flops 1310726 | bytes 2621556 | solution.py:768
  128.2 10.4 %branch_0_fun.2 = bf16[640,256]{1,0:T(8,128)(2,1)} custom-call(s32[1]{0:T(128)} %bitcast.off_ref, bf16[1280,256]{1,0:T(8,128)(2,1)S(1)} %get-tuple-element.15.q_ref, bf16[2,10240,128]{2,1,0:T(8,128)(2,1)} %get-tuple-element.16.kv_ref, f32[1280,128]{1,0:T(8,128)S(1)} %get-tuple-element.17.lim_ref), custom_call_target="tpu_custom_call" | custom-call | tf_op jit(solution)/shard_map/cond/branch_0_fun/pallas_call | solution.py:739
  138.6 70.8 %collective-permute-start = (bf16[640,256]{1,0:T(8,128)(2,1)}, bf16[640,256]{1,0:T(8,128)(2,1)S(1)}, u32[]{:S(2)}, u32[]{:S(2)}) collective-permute-start(bf16[640,256]{1,0:T(8,128)(2,1)} %branch_0_fun.2), channel_id=1, source_target_pairs={{0,112},{16,96},{32,80},{48,64},{64,48},{80,32},{96,16},{112,0},{1... | collective-permute-start | bytes 983048 | tf_op jit(solution)/shard_map/cond/branch_0_fun/ppermute | solution.py:759
  209.4 84.5 %branch_0_fun.3 = bf16[640,256]{1,0:T(8,128)(2,1)} custom-call(s32[1]{0:T(128)} %bitcast.1.off_ref, bf16[1280,256]{1,0:T(8,128)(2,1)S(1)} %get-tuple-element.15.q_ref, bf16[2,10240,128]{2,1,0:T(8,128)(2,1)} %get-tuple-element.16.kv_ref, f32[1280,128]{1,0:T(8,128)S(1)} %get-tuple-element.17.lim_ref), custom_call_target="tpu_custom_call" | custom-call | tf_op jit(solution)/shard_map/cond/branch_0_fun/pallas_call | solution.py:739
  293.9 0.0 collective-permute-done
  293.9 1.0 pad_maximum_fusion
  294.9 0.8 copy.13
Async XLA Ops:
  138.6 155.3 %collective-permute-start = (bf16[640,256]{1,0:T(8,128)(2,1)}, bf16[640,256]{1,0:T(8,128)(2,1)S(1)}, u32[]{:S(2)}, u32[]{:S(2)}) collective-permute-start(bf16[640,256]{1,0:T(8,128)(2,1)} %branch_0_fun.2), channel_id=1, source_target_pairs={{0,112},{16,96},{32,80},{48,64},{64,48},{80,32},{96,16},{112,0},{1... | collective-permute-start | bytes 983048 | tf_op jit(solution)/shard_map/cond/branch_0_fun/ppermute | solution.py:759

commit v6 on v5

--- a/solution.py
+++ b/solution.py
@@ -11,7 +11,7 @@
 HD = 128
 EPS = 1e-05
 CHUNK = 128
-LAG = 1
+LAG = 0
 MESH = pl.DeviceIdType.MESH
 NEG = -1e30
 SAFE = 64.0
@@ -24,11 +24,11 @@
 
 def project_kernel(
     side, count_ref, gap_ref, text_ref, visual_ref, gain_ref, wq_ref, wkv_ref,
-    q_out, kv_out, lim_out, peak,
+    q_out, kv_out, lim_out, peak_out,
     before, scales, wsend, wall, seen, picked, landed, slots, lims, xall, psend_k, psend_q, pmid_k,
-    pmid_q, precv_k, precv_q, squares, sqrecv, factors, qown,
+    pmid_q, precv_k, precv_q, squares, sqrecv, factors, qown, peak, peaks,
     vis_s, vis_r, blk_s, blk_r, w_s, w_r, wp_s, wp_r, wr_s, wr_r, x_s, x_r, xf_s, xf_r, p_s, p_r, pf_s, pf_r,
-    n_s, n_r, kx_s, kx_r, ky_s, ky_r, kc_s, kc_r, q_s, q_r,
+    n_s, n_r, kx_s, kx_r, ky_s, ky_r, kc_s, kc_r, q_s, q_r, m_s, m_r,
 ):
     seq_count, enc_count = lax.axis_size("seq"), lax.axis_size("enc")
     s, e = lax.axis_index("seq"), lax.axis_index("enc")
@@ -357,7 +357,28 @@
 
     def record(i, norm):
         wide = jnp.broadcast_to(norm, (CHUNK, HD)).reshape(CHUNK // 8, 8, HD)
-        peak[i] = jnp.maximum(peak[i], jnp.max(wide, axis=0))
+        peak[0, i] = jnp.maximum(peak[0, i], jnp.max(wide, axis=0))
+
+    def meet(step, k):
+        return send(
+            peak.at[step], peaks.at[step, k], m_s.at[step, k], m_r.at[step, k],
+            s, along(k) if step else across(k),
+        )
+
+    def climb(step, c):
+        @pl.when(c == chunks - 1)
+        def _():
+            if step > 0:
+                highest = peak[step - 1]
+                for k in range(1, side):
+                    meet(step - 1, k).wait_recv()
+                    highest = jnp.maximum(highest, peaks[step - 1, k])
+                if step == 2:
+                    peak_out[...] = highest
+                    return
+                peak[step] = highest
+            for k in range(1, side):
+                meet(step, k).start()
 
     def finish_keys(c):
         total = total_of(KEYS, c)
@@ -408,9 +429,11 @@
     behind = LAG
     stages = (
         push, hop, multiply, multiply_queries, functools.partial(merge, KEYS),
-        functools.partial(merge, QUERIES), finish_keys, spread_out, finish_queries, hand_over,
+        functools.partial(merge, QUERIES), finish_keys, spread_out, finish_queries,
+        functools.partial(climb, 0), functools.partial(climb, 1), hand_over,
+        functools.partial(climb, 2),
     )
-    lags = (0, 2, 3, 3 + behind, 4, 4 + behind, 5, 6, 5 + behind, 8)
+    lags = (0, 2, 3, 3 + behind, 4, 4 + behind, 5, 6, 5 + behind, 5 + behind, 6 + behind, 8, 8)
     peak[...] = jnp.zeros_like(peak)
 
     @pl.loop(0, chunks + max(lags))
@@ -439,6 +462,10 @@
     @pl.loop(0, chunks // 2)
     def _(c):
         trade(c).wait()
+
+    for step in range(2):
+        for k in range(1, side):
+            meet(step, k).wait_send()
 
     @pl.loop(1, side)
     def _(k):
@@ -504,6 +531,8 @@
             VMEM((side, chunks, 8, CHUNK), f32),
             VMEM((rows, HD), f32),
             VMEM((rows, q_columns), bf16),
+            VMEM((2, 2, 8, HD), f32),
+            VMEM((2, side, 2, 8, HD), f32),
             *dma(enc_count),
             *dma(seq_count),
             *dma(side),
@@ -518,6 +547,7 @@
             *dma(ys, chunks),
             *dma(ys, chunks),
             *dma(chunks),
+            *dma(2, side),
         ],
         compiler_params=pltpu.CompilerParams(
             collective_id=0, has_side_effects=True, vmem_limit_bytes=60 << 20
@@ -541,8 +571,8 @@
 
 
 def quick_kernel(
-    bk, side, q_ref, kv_ref, lim_ref, top_ref, o_ref, safe_ref,
-    kv, lent, acc, den, peak, peaks, kv_s, o_s, o_r, m_s, m_r,
+    bk, cuts, q_ref, kv_ref, lim_ref, top_ref, o_ref, safe_ref,
+    kv, lent, acc, den, peaks, kv_s, o_s, o_r, m_s, m_r,
 ):
     s, e = lax.axis_index("seq"), lax.axis_index("enc")
     seq_count = lax.axis_size("seq")
@@ -561,47 +591,23 @@
         load(j).start()
 
     barrier = pltpu.get_barrier_semaphore()
-    z, x = e // side, e % side
-    sizes = (side, side, seq_count)
-
-    def goal(step, k):
-        if step == 0:
-            return s, z * side + (x + k) % side
-        if step == 1:
-            return s, ((z + k) % side) * side + x
-        return (s + k) % seq_count, e
-
-    for step, size in enumerate(sizes):
-        for k in range(1, size):
-            pl.semaphore_signal(barrier, inc=1, device_id=goal(step, k), device_id_type=MESH)
-
-    peak[0] = top_ref[...]
-
-    def meet(step, k):
+
+    @pl.loop(1, seq_count)
+    def _(k):
+        pl.semaphore_signal(barrier, inc=1, device_id=((s + k) % seq_count, e), device_id_type=MESH)
+
+    def meet(k):
         return pltpu.make_async_remote_copy(
-            src_ref=peak.at[step], dst_ref=peaks.at[step, k], send_sem=m_s.at[step, k],
-            recv_sem=m_r.at[step, k], device_id=goal(step, k), device_id_type=MESH,
-        )
-
-    def climb(step):
-        if step > 0:
-            highest = peak[step - 1]
-            for k in range(1, sizes[step - 1]):
-                meet(step - 1, k).wait_recv()
-                highest = jnp.maximum(highest, peaks[step - 1, k])
-            if step == len(sizes):
-                bound = jnp.max(highest[0]) * jnp.max(highest[1])
-                safe_ref[0] = jnp.where(bound < SAFE * SAFE, 1, 0).astype(jnp.int32)
-                return
-            peak[step] = highest
-        for k in range(1, sizes[step]):
-            meet(step, k).start()
-
-    def job(part, first, ready, target, base, hook):
-        size = half
-        rows_here = pl.ds(part * half, half)
-        acc[...] = jnp.zeros_like(acc)
-        den[...] = jnp.zeros_like(den)
+            src_ref=top_ref, dst_ref=peaks.at[k], send_sem=m_s.at[k], recv_sem=m_r.at[k],
+            device_id=((s + k) % seq_count, e), device_id_type=MESH,
+        )
+
+    def job(begin, end, first, ready, target):
+        size = end - begin
+        here = pl.ds(begin, size)
+        part = pl.ds(0, size)
+        acc[:, part] = jnp.zeros((heads, size, HD), jnp.float32)
+        den[:, part] = jnp.zeros((heads, size, HD), jnp.float32)
         whole = first // bk
         last = jnp.minimum((first + size + 255 + bk - 1) // bk, blocks)
 
@@ -612,59 +618,73 @@
 
             key = pl.multiple_of(j * bk, bk)
             keys, values = kv[0, pl.ds(key, bk), :], kv[1, pl.ds(key, bk), :]
-            lim = lim_ref[rows_here, :] if masked else None
+            lim = lim_ref[here, :] if masked else None
             for head in range(heads):
-                q = q_ref[rows_here, head * HD : (head + 1) * HD]
+                q = q_ref[here, head * HD : (head + 1) * HD]
                 p = jnp.exp2(masked_scores(q, keys, lim, key))
-                acc[head] += jnp.dot(
+                acc[head, part] += jnp.dot(
                     p.astype(jnp.bfloat16), values, preferred_element_type=jnp.float32
                 )
-                den[head] += lane_sums(p)
+                den[head, part] += lane_sums(p)
 
         @pl.loop(0, whole)
         def _(j):
             step(j, False)
 
-        hook(1)
-
         @pl.loop(whole, last)
         def _(j):
             step(j, True)
 
-        hook(2)
         for head in range(heads):
-            result = acc[head] / jnp.sum(den[head], axis=1, keepdims=True)
-            target[base : base + half, head * HD : (head + 1) * HD] = result.astype(jnp.bfloat16)
-        return last
-
-    used = job(0, other * rows, 0, lent, 0, lambda step: None)
-    pl.semaphore_wait(barrier, sum(sizes) - len(sizes))
-    back = pltpu.make_async_remote_copy(
-        src_ref=lent, dst_ref=o_ref.at[pl.ds(0, half)], send_sem=o_s, recv_sem=o_r,
-        device_id=(other, e), device_id_type=MESH,
-    )
-    back.start()
-    climb(0)
-    used = jnp.maximum(used, job(1, s * rows + half, used, o_ref, half, climb))
+            result = acc[head, part] / jnp.sum(den[head, part], axis=1, keepdims=True)
+            target[here, head * HD : (head + 1) * HD] = result.astype(jnp.bfloat16)
+        return jnp.maximum(ready, last)
+
+    def back(i):
+        here = pl.ds(cuts[i], cuts[i + 1] - cuts[i])
+        return pltpu.make_async_remote_copy(
+            src_ref=lent.at[here], dst_ref=o_ref.at[here], send_sem=o_s.at[i], recv_sem=o_r.at[i],
+            device_id=(other, e), device_id_type=MESH,
+        )
+
+    used = jnp.int32(0)
+    for i in range(len(cuts) - 1):
+        used = job(cuts[i], cuts[i + 1], other * rows + cuts[i], used, lent)
+        if i == 0:
+            pl.semaphore_wait(barrier, seq_count - 1)
+
+            @pl.loop(1, seq_count)
+            def _(k):
+                meet(k).start()
+
+        back(i).start()
+    used = job(half, rows, s * rows + half, used, o_ref)
 
     @pl.loop(used, blocks)
     def _(j):
         load(j).wait()
 
-    climb(3)
-    back.wait()
-    for step, size in enumerate(sizes):
-        for k in range(1, size):
-            meet(step, k).wait_send()
+    highest = top_ref[...]
+    for k in range(1, seq_count):
+        meet(k).wait_recv()
+        highest = jnp.maximum(highest, peaks[k])
+    bound = jnp.max(highest[0]) * jnp.max(highest[1])
+    safe_ref[0] = jnp.where(bound < SAFE * SAFE, 1, 0).astype(jnp.int32)
+    for i in range(len(cuts) - 1):
+        back(i).wait()
+
+    @pl.loop(1, seq_count)
+    def _(k):
+        meet(k).wait_send()
 
 
 def quick(query, keyval, lim, peak):
     rows, width = query.shape
     seq_count = lax.axis_size("seq")
-    side = math.isqrt(lax.axis_size("enc"))
     heads, bk = width // HD, 1024
+    cuts = (0, 384, rows // 2)
     return pl.pallas_call(
-        functools.partial(quick_kernel, bk, side),
+        functools.partial(quick_kernel, bk, cuts),
         out_shape=(
             jax.ShapeDtypeStruct((rows, width), jnp.bfloat16),
             jax.ShapeDtypeStruct((1,), jnp.int32),
@@ -681,13 +701,12 @@
             VMEM((rows // 2, width), jnp.bfloat16),
             VMEM((heads, rows // 2, HD), jnp.float32),
             VMEM((heads, rows // 2, HD), jnp.float32),
-            VMEM((3, 2, 8, HD), jnp.float32),
-            VMEM((3, seq_count, 2, 8, HD), jnp.float32),
+            VMEM((seq_count, 2, 8, HD), jnp.float32),
             pltpu.SemaphoreType.DMA((keyval.shape[1] // bk,)),
-            pltpu.SemaphoreType.DMA,
-            pltpu.SemaphoreType.DMA,
-            pltpu.SemaphoreType.DMA((3, seq_count)),
-            pltpu.SemaphoreType.DMA((3, seq_count)),
+            pltpu.SemaphoreType.DMA((len(cuts) - 1,)),
+            pltpu.SemaphoreType.DMA((len(cuts) - 1,)),
+            pltpu.SemaphoreType.DMA((seq_count,)),
+            pltpu.SemaphoreType.DMA((seq_count,)),
         ],
         compiler_params=pltpu.CompilerParams(
             collective_id=1, has_side_effects=True, vmem_limit_bytes=56 << 20

time: 296 us -> 293 us (0.990)
  Pallas kernels: 223 us -> 218 us
    pallas_call x1, Pallas kernels: 29.6 us -> 24.9 us  [quick(): pl.pallas_call(functools.partial(quick_kernel, bk, cuts), out_shape=(jax....]
where the time goes in v6:
time: 293 us; the launch traced here: 292 us
  Pallas kernels  218 us (74%)
  starting transfers between devices  72 us (25%)
    pallas_call x1, Pallas kernels, project(): pl.pallas_call(functools.partial(project_kernel, side), out_shape=(jax.Sh...  98.1 us
    pallas_call x2, Pallas kernels, attend(): pl.pallas_call(functools.partial(careful_kernel, bq, bk), out_shape=jax.S...  94.9 us
    ppermute x1, starting transfers between devices, careful(): lax.ppermute(lent, 'seq', [(i, seq_count - 1 - i) for i in range(seq_coun...  72 us
    pallas_call x1, Pallas kernels, quick(): pl.pallas_call(functools.partial(quick_kernel, bk, cuts), out_shape=(jax....  24.9 us
  transfers between devices with their start and end apart: 1, of which 0 were waited for; matrix products, arithmetic and copies ran while one was open for 0% of the time, Pallas kernels for 29%

profile of v6, /device:TPU:25, one launch (start us, length us, event | category | flops | bytes accessed | tf_op | source)
XLA Modules:
  0.0 292.5 jit_solution(7949426532163037727)
XLA Ops:
  0.0 98.1 %shard_map.75 = (bf16[1280,256]{1,0:T(8,128)(2,1)S(1)}, bf16[2,10240,128]{2,1,0:T(8,128)(2,1)}, f32[1280,128]{1,0:T(8,128)S(1)}, f32[2,8,128]{2,1,0:T(8,128)}) custom-call(s32[32]{0:T(128)} %count_ref.1, s32[33]{0:T(128)} %gap_ref.1, bf16[1280,256]{1,0:T(8,128)(2,1)} %text_ref.1, bf16[40,4096]{1,0:T(8,128)(2,1)} %visual_ref.1, bf16[256]{0:T(256)(128)(2,1)} %gain_ref.1, ...), custom_call_target="tpu_custom_call" | custom-call | tf_op jit(solution)/shard_map/pallas_call | solution.py:501
  98.2 24.9 %shard_map.76 = (bf16[1280,256]{1,0:T(8,128)(2,1)S(1)}, s32[1]{0:T(128)}) custom-call(bf16[1280,256]{1,0:T(8,128)(2,1)S(1)} %get-tuple-element.24.q_ref, bf16[2,10240,128]{2,1,0:T(8,128)(2,1)} %get-tuple-element.25.kv_ref, f32[1280,128]{1,0:T(8,128)S(1)} %get-tuple-element.26.lim_ref, f32[2,8,128]{2,1,0:T(8,128)} %get-tuple-element.27.top_ref), custom_call_target="tpu_custom_call" | custom-call | tf_op jit(solution)/shard_map/pallas_call | solution.py:686
  123.7 167.9 %conditional.1 = (bf16[1280,256]{1,0:T(8,128)(2,1)S(1)}) conditional(s32[]{:T(128)} %bitcast.2, (bf16[1280,256]{1,0:T(8,128)(2,1)S(1)}, bf16[2,10240,128]{2,1,0:T(8,128)(2,1)}, f32[1280,128]{1,0:T(8,128)S(1)}) %tuple.11, bf16[1280,256]{1,0:T(8,128)(2,1)S(1)} %get-tuple-element.29), branch_computations={%region_0.0_spmd, %region_1.0_spmd} | conditional | flops 1310726 | bytes 2621556 | solution.py:787
  123.7 10.4 %branch_0_fun.2 = bf16[640,256]{1,0:T(8,128)(2,1)} custom-call(s32[1]{0:T(128)} %bitcast.off_ref, bf16[1280,256]{1,0:T(8,128)(2,1)S(1)} %get-tuple-element.15.q_ref, bf16[2,10240,128]{2,1,0:T(8,128)(2,1)} %get-tuple-element.16.kv_ref, f32[1280,128]{1,0:T(8,128)S(1)} %get-tuple-element.17.lim_ref), custom_call_target="tpu_custom_call" | custom-call | tf_op jit(solution)/shard_map/cond/branch_0_fun/pallas_call | solution.py:758
  134.1 72.0 %collective-permute-start = (bf16[640,256]{1,0:T(8,128)(2,1)}, bf16[640,256]{1,0:T(8,128)(2,1)S(1)}, u32[]{:S(2)}, u32[]{:S(2)}) collective-permute-start(bf16[640,256]{1,0:T(8,128)(2,1)} %branch_0_fun.2), channel_id=1, source_target_pairs={{0,112},{16,96},{32,80},{48,64},{64,48},{80,32},{96,16},{112,0},{1... | collective-permute-start | bytes 983048 | tf_op jit(solution)/shard_map/cond/branch_0_fun/ppermute | solution.py:778
  206.1 84.5 %branch_0_fun.3 = bf16[640,256]{1,0:T(8,128)(2,1)} custom-call(s32[1]{0:T(128)} %bitcast.1.off_ref, bf16[1280,256]{1,0:T(8,128)(2,1)S(1)} %get-tuple-element.15.q_ref, bf16[2,10240,128]{2,1,0:T(8,128)(2,1)} %get-tuple-element.16.kv_ref, f32[1280,128]{1,0:T(8,128)S(1)} %get-tuple-element.17.lim_ref), custom_call_target="tpu_custom_call" | custom-call | tf_op jit(solution)/shard_map/cond/branch_0_fun/pallas_call | solution.py:758
  290.6 0.0 collective-permute-done
  290.6 1.0 pad_maximum_fusion
  291.6 0.8 copy.13
Async XLA Ops:
  134.1 156.5 %collective-permute-start = (bf16[640,256]{1,0:T(8,128)(2,1)}, bf16[640,256]{1,0:T(8,128)(2,1)S(1)}, u32[]{:S(2)}, u32[]{:S(2)}) collective-permute-start(bf16[640,256]{1,0:T(8,128)(2,1)} %branch_0_fun.2), channel_id=1, source_target_pairs={{0,112},{16,96},{32,80},{48,64},{64,48},{80,32},{96,16},{112,0},{1... | collective-permute-start | bytes 983048 | tf_op jit(solution)/shard_map/cond/branch_0_fun/ppermute | solution.py:778
